TPU v7x, 32 devices: a whole 2x2x4 slice. The times are simulated.
32 devices in a mesh: mesh: 16 (over z, y, core), band: 2 (over x).
Axes of the slice: x: 2, y: 2, z: 4, core: 2. Of those that a mesh axis runs over, the one named last changes fastest.
Arguments:
- psi: bfloat16 [16, 286720], P('band', 'mesh'), may hold values from -9 to 9
- cell_nodes: int32 [216, 128], replicated, may hold values from 0 to 19711, as said below
- cell_scale: float32 [2048], P('mesh'), may hold values from 0.5 to 2
- cell_matrix: bfloat16 [216, 216], replicated, may hold values from -1 to 2
- node_potential: bfloat16 [286720], P('mesh'), may hold values from -1.5 to 0.5
- proj_values: bfloat16 [216, 8, 2048], P(None, None, 'mesh'), may hold values from -1 to 1
- entry_cell: int32 [2048], P('mesh'), may hold values from 0 to 127
- entry_atom: int32 [2048], P('mesh'), may hold values from -1 to 191, as said below
- coupling: float32 [1024, 8, 8], P('mesh'), may hold values from -3 to 3
Outputs:
- filtered: bfloat16 [16, 286720], P('band', 'mesh')
- correlation: float32 [16, 16], replicated
Inputs may be any that keep to these rules, and one draw needn't show every extreme that they name: `cell_nodes`: node j = 36 a + 6 b + c of a cell is its local node (a, b, c) in the order the cell_matrix uses; cells that share a node give it the same number; values 17920 + i name node i of the next partition, and only nodes below 1792 of a partition are named so by the previous one. `entry_atom`: live entries of a partition come first, then -1 padding; the number of live entries differs between partitions.
All inputs are finite; a program needn't handle non-finite values.
Results may differ from a plain program's by a relative error of at most 0.0022.
Values may be sent and summed in bfloat16 or wider, within the bound.
A program may use at most 128 MiB of HBM per device.

v0:
```python
import jax
import jax.numpy as jnp
from jax import lax
from jax.experimental import pallas as pl
from jax.experimental.pallas import tpu as pltpu
from jax.sharding import PartitionSpec as P

FACEP = 1792
CENTER = 0.5
HALFWIDTH = 2.5
HIGH = lax.Precision.HIGHEST
WIDE = 256
GROUP = 36
F32 = jnp.float32
BF16 = jnp.bfloat16


def fill_onehot(cn_ref, group, oh_ref):
    rows = cn_ref[group]
    hi = jnp.bitwise_and(rows, WIDE - 1)
    lanes = rows.shape[1]
    iota = lax.broadcasted_iota(jnp.int32, (WIDE, lanes), 0)
    for jj in range(GROUP):
        oh_ref[:, jj * lanes:(jj + 1) * lanes] = jnp.where(
            iota == hi[jj:jj + 1, :], 1.0, 0.0
        ).astype(BF16)
    return lax.shift_right_logical(rows, 8)


def gather_kernel(sched_ref, cn_ref, ext_ref, xs_ref, lhs_ref, oh_ref):
    states = ext_ref.shape[0]
    chunks = lhs_ref.shape[0] - 1
    layers = ext_ref.shape[1] // (chunks * WIDE)
    groups = cn_ref.shape[0]
    cells = cn_ref.shape[2]
    padded = lhs_ref.shape[1]
    slots = sched_ref.shape[0] // groups
    lhs_ref[...] = jnp.zeros_like(lhs_ref)
    for c in range(chunks):
        base = c * layers * WIDE
        parts = [
            ext_ref[:, base + l * WIDE:base + (l + 1) * WIDE].astype(F32) for l in range(layers)
        ]
        parts.append(jnp.zeros((padded - layers * states, WIDE), F32))
        lhs_ref[c] = jnp.concatenate(parts, axis=0).astype(BF16)
    xs_ref[...] = jnp.zeros_like(xs_ref)

    def group_body(g, carry):
        lo = fill_onehot(cn_ref, g, oh_ref)

        def pair_body(r, inner):
            first = sched_ref[g * slots + 2 * r]
            second = sched_ref[g * slots + 2 * r + 1]
            lhs = jnp.concatenate([lhs_ref[first], lhs_ref[second]], axis=0)
            out = jnp.dot(lhs, oh_ref[...], preferred_element_type=F32)
            for jj in range(GROUP):
                where = pl.ds(pl.multiple_of((g * GROUP + jj) * states, states), states)
                value = xs_ref[where, :]
                lanes = slice(jj * cells, (jj + 1) * cells)
                for half, chunk in enumerate((first, second)):
                    row = lo[jj:jj + 1, :] - chunk * layers
                    for l in range(layers):
                        at = half * padded + l * states
                        value = jnp.where(row == l, out[at:at + states, lanes], value)
                xs_ref[where, :] = value
            return inner

        pairs = lax.shift_right_logical(sched_ref[g * slots + slots - 1] + 1, 1)
        return lax.fori_loop(0, pairs, pair_body, carry)

    lax.fori_loop(0, groups, group_body, 0)


def scatter_kernel(sched_ref, cn_ref, ct_ref, coef_ref, coup_ref, proj_ref, ecell_ref,
                   eatom_ref, y_ref, oh_ref, ns_ref, v_ref, lhs_ref, acc_ref):
    chunks, rows_in_chunk, _ = acc_ref.shape
    chunks = chunks - 1
    groups = cn_ref.shape[0]
    cells = cn_ref.shape[2]
    width = groups * GROUP
    states = ct_ref.shape[0] // width
    layers = rows_in_chunk // (2 * states)
    nproj = proj_ref.shape[1]
    entries = ecell_ref.shape[1]
    atoms = coef_ref.shape[2]
    slot_ids = lax.broadcasted_iota(jnp.int32, (atoms, entries), 0)
    entry_terms = jnp.zeros((nproj * states, entries), F32)
    for g in range(3):
        rows = []
        for k in range(nproj):
            acc = jnp.zeros((states, atoms), F32)
            for l in range(nproj):
                acc = acc + (
                    coup_ref[g, k * nproj + l:k * nproj + l + 1, :]
                    * coef_ref[g, l * states:(l + 1) * states, :]
                )
            rows.append(acc)
        chosen = jnp.where(eatom_ref[...] == slot_ids + g * atoms, 1.0, 0.0)
        entry_terms = entry_terms + jnp.dot(
            jnp.concatenate(rows, axis=0), chosen, precision=HIGH, preferred_element_type=F32
        )
    terms = [entry_terms[k * states:(k + 1) * states, :] for k in range(nproj)]

    def node_body(j, carry):
        proj = proj_ref[j].astype(F32)
        total = proj[0:1, :] * terms[0]
        for k in range(1, nproj):
            total = total + proj[k:k + 1, :] * terms[k]
        ns_ref[pl.ds(pl.multiple_of(j * states, states), states), :] = total
        return carry

    lax.fori_loop(0, width, node_body, 0, unroll=8)
    cell_ids = lax.broadcasted_iota(jnp.int32, (cells, entries), 0)
    spread = jnp.where(cell_ids == ecell_ref[...], 1.0, 0.0).astype(BF16)
    back = (((1,), (1,)), ((), ()))
    node_vals = ns_ref[...]
    node_top = node_vals.astype(BF16)
    node_rest = (node_vals - node_top.astype(F32)).astype(BF16)
    v_ref[...] = (
        ct_ref[...]
        + lax.dot_general(node_top, spread, back, preferred_element_type=F32)
        + lax.dot_general(node_rest, spread, back, preferred_element_type=F32)
    )
    acc_ref[...] = jnp.zeros_like(acc_ref)
    slots = sched_ref.shape[0] // groups

    def group_body(g, carry):
        lo = fill_onehot(cn_ref, g, oh_ref)

        def pair_body(r, inner):
            first = sched_ref[g * slots + 2 * r]
            second = sched_ref[g * slots + 2 * r + 1]
            for jj in range(GROUP):
                start = pl.multiple_of((g * GROUP + jj) * states, states)
                value = v_ref[pl.ds(start, states), :]
                top = value.astype(BF16).astype(F32)
                both = jnp.concatenate([top, value - top], axis=0)
                lanes = slice(jj * cells, (jj + 1) * cells)
                for half, chunk in enumerate((first, second)):
                    row = lo[jj:jj + 1, :] - chunk * layers
                    for l in range(layers):
                        at = half * rows_in_chunk + l * 2 * states
                        lhs_ref[at:at + 2 * states, lanes] = (
                            jnp.where(row == l, both, 0.0).astype(BF16)
                        )
            out = lax.dot_general(lhs_ref[...], oh_ref[...], back, preferred_element_type=F32)
            acc_ref[first] += out[:rows_in_chunk]
            acc_ref[second] += out[rows_in_chunk:]
            return inner

        pairs = lax.shift_right_logical(sched_ref[g * slots + slots - 1] + 1, 1)
        return lax.fori_loop(0, pairs, pair_body, carry)

    lax.fori_loop(0, groups, group_body, 0)
    for c in range(chunks):
        for l in range(layers):
            base = (c * layers + l) * WIDE
            at = l * 2 * states
            y_ref[:, base:base + WIDE] = (
                acc_ref[c, at:at + states, :] + acc_ref[c, at + states:at + 2 * states, :]
            )


MESH_ID = pl.DeviceIdType.MESH


def ring_peer(steps):
    count = lax.axis_size("mesh")
    return lax.rem(lax.axis_index("mesh") + steps + count, count)


def send(src, dst, sems, at, peer):
    copy = pltpu.make_async_remote_copy(
        src_ref=src, dst_ref=dst, send_sem=sems.at[0, at], recv_sem=sems.at[1, at],
        device_id=peer, device_id_type=MESH_ID,
    )
    copy.start()
    return copy


def greet(peers):
    barrier = pltpu.get_barrier_semaphore()
    for peer in peers:
        pl.semaphore_signal(barrier, inc=1, device_id=peer, device_id_type=MESH_ID)
    return barrier


def start_kernel(psi_ref, pot_ref, coup_ref, ext_ref, potx_ref, coups_ref, sems):
    count = psi_ref.shape[1]
    face = ext_ref.shape[1] - count
    ahead, behind = {"mesh": ring_peer(1)}, {"mesh": ring_peer(-1)}
    pl.semaphore_wait(greet((ahead, behind)), 2)
    copies = [
        send(psi_ref.at[:, :face], ext_ref.at[:, count:], sems, 0, behind),
        send(coup_ref, coups_ref.at[0], sems, 1, ahead),
        send(coup_ref, coups_ref.at[2], sems, 2, behind),
        send(pot_ref.at[:, :face], potx_ref.at[:, count:], sems, 3, behind),
    ]
    ext_ref[:, :count] = psi_ref[...]
    potx_ref[:, :count] = pot_ref[...]
    coups_ref[1] = coup_ref[...]
    for copy in copies:
        copy.wait()


def atoms_kernel(xs_ref, kmat_ref, scale_ref, proj_ref, ecell_ref, eatom_ref, ct_ref, coef_ref,
                 es_ref, grouped_ref, left_ref, right_ref, far_ref, sems):
    peers = [{"mesh": ring_peer(steps)} for steps in (1, -1, 2, -2)]
    barrier = greet(peers)
    width, nproj, entries = proj_ref.shape
    cells = xs_ref.shape[1]
    states = xs_ref.shape[0] // width
    cell_ids = lax.broadcasted_iota(jnp.int32, (cells, entries), 0)
    spread = jnp.where(cell_ids == ecell_ref[...], 1.0, 0.0).astype(BF16)
    es_ref[...] = jnp.dot(xs_ref[...].astype(BF16), spread, preferred_element_type=F32)

    def partial_body(j, accs):
        values = es_ref[pl.ds(pl.multiple_of(j * states, states), states), :]
        proj = proj_ref[j].astype(F32)
        return tuple(acc + proj[k:k + 1, :] * values for k, acc in enumerate(accs))

    zero = jnp.zeros((states, entries), F32)
    accs = lax.fori_loop(0, width, partial_body, (zero,) * nproj, unroll=8)
    partial_sum = jnp.concatenate(accs, axis=0)
    atoms = grouped_ref.shape[2]
    slot_ids = lax.broadcasted_iota(jnp.int32, (atoms, entries), 0)
    for g in range(3):
        chosen = jnp.where(eatom_ref[...] == slot_ids + g * atoms, 1.0, 0.0)
        grouped_ref[g] = lax.dot_general(
            partial_sum, chosen, (((1,), (1,)), ((), ())), precision=HIGH,
            preferred_element_type=F32,
        )
    pl.semaphore_wait(barrier, 4)
    copies = [
        send(grouped_ref.at[1:3], left_ref, sems, 0, peers[0]),
        send(grouped_ref.at[0:2], right_ref, sems, 1, peers[1]),
        send(grouped_ref.at[2], far_ref.at[0], sems, 2, peers[2]),
        send(grouped_ref.at[0], far_ref.at[1], sems, 3, peers[3]),
    ]
    kmat = kmat_ref[...]
    scale = scale_ref[...]
    for s in range(0, states, 2):
        pair = jnp.concatenate(
            [xs_ref[pl.ds(s, width, stride=states), :], xs_ref[pl.ds(s + 1, width, stride=states), :]],
            axis=1,
        ).astype(BF16)
        out = jnp.dot(kmat, pair, preferred_element_type=F32)
        ct_ref[pl.ds(s, width, stride=states), :] = out[:, :cells] * scale
        ct_ref[pl.ds(s + 1, width, stride=states), :] = out[:, cells:] * scale
    for copy in copies:
        copy.wait()
    coef_ref[0] = left_ref[0] + far_ref[0] + grouped_ref[0]
    coef_ref[1] = grouped_ref[1] + left_ref[1] + right_ref[0]
    coef_ref[2] = right_ref[1] + grouped_ref[2] + far_ref[1]


def first_kernel(y_ref, ext_ref, pot_ref, first_ref, low_ref, high_ref, sems):
    full = y_ref.shape[1]
    face = low_ref.shape[1]
    count = full - face
    ahead, behind = {"mesh": ring_peer(1)}, {"mesh": ring_peer(-1)}
    barrier = greet((ahead, behind))

    def finish(total, at):
        scaled = (total + pot_ref[:, at] * ext_ref[:, at].astype(F32)) / HALFWIDTH
        first_ref[:, at] = scaled.astype(BF16)

    middle = face * (1 + (count // face - 1) // 2)
    for base in range(face, middle, face):
        at = slice(base, base + face)
        finish(y_ref[:, at], at)
    pl.semaphore_wait(barrier, 2)
    copies = [
        send(y_ref.at[:, count:], low_ref, sems, 0, ahead),
        send(y_ref.at[:, :face], high_ref, sems, 1, behind),
    ]
    for base in range(middle, count, face):
        at = slice(base, base + face)
        finish(y_ref[:, at], at)
    for copy in copies:
        copy.wait()
    finish(y_ref[:, :face] + low_ref[...], slice(0, face))
    finish(y_ref[:, count:] + high_ref[...], slice(count, full))


def last_kernel(y_ref, first_ref, psi_ref, pot_ref, out_ref, corr_ref, low_ref, other_ref,
                slots_ref, sems):
    count = psi_ref.shape[1]
    face = low_ref.shape[1]
    devices = lax.axis_size("mesh")
    bands = lax.axis_size("band")
    me = lax.axis_index("mesh")
    band = lax.axis_index("band")
    partner = {"band": lax.rem(band + 1, bands)}
    barrier = greet((partner,))

    def greet_body(steps, carry):
        pl.semaphore_signal(
            barrier, inc=1, device_id={"mesh": lax.rem(me + steps, devices)}, device_id_type=MESH_ID
        )
        return carry

    lax.fori_loop(1, devices, greet_body, 0)

    def finish(total, at):
        scaled = (total + pot_ref[:, at] * first_ref[:, at].astype(F32)) / HALFWIDTH
        out_ref[:, at] = (2.0 * scaled - psi_ref[:, at].astype(F32)).astype(BF16)

    for base in range(face, count, face):
        at = slice(base, base + face)
        finish(y_ref[:, at], at)
    pl.semaphore_wait(barrier, devices)
    tail = send(y_ref.at[:, count:count + face], low_ref, sems, 0, {"mesh": ring_peer(1)})
    swap = send(out_ref.at[:, face:], other_ref.at[:, face:], sems, 1, partner)
    states = out_ref.shape[0]

    def gram(base):
        at = slice(base, base + face)
        own, other = out_ref[:, at].astype(F32), other_ref[:, at].astype(F32)
        block = jnp.concatenate(
            [jnp.where(band == 0, own, other), jnp.where(band == 0, other, own)], axis=0
        ).astype(BF16)
        return lax.dot_general(
            block, block, (((1,), (1,)), ((), ())), preferred_element_type=F32
        )

    swap.wait()
    total = gram(face)
    for base in range(2 * face, count, face):
        total = total + gram(base)
    tail.wait()
    finish(y_ref[:, :face] + low_ref[...], slice(0, face))
    edge = send(out_ref.at[:, :face], other_ref.at[:, :face], sems, 3, partner)
    edge.wait()
    total = total + gram(0)
    slots_ref[me] = total

    def push(steps, carry):
        send(slots_ref.at[me], slots_ref.at[me], sems, 2, {"mesh": lax.rem(me + steps, devices)})
        return carry

    lax.fori_loop(1, devices, push, 0)
    pltpu.make_async_remote_copy(
        src_ref=slots_ref.at[pl.ds(0, devices - 1)], dst_ref=slots_ref.at[pl.ds(0, devices - 1)],
        send_sem=sems.at[0, 2], recv_sem=sems.at[1, 2], device_id=partner, device_id_type=MESH_ID,
    ).wait()
    corr_ref[...] = jnp.sum(slots_ref[...], axis=0) * (1.0 / (devices * count))


def local(
    psi,
    cell_nodes,
    cell_scale,
    cell_matrix,
    node_potential,
    proj_values,
    entry_cell,
    entry_atom,
    coupling,
):
    states, node_count = psi.shape
    width, cells = cell_nodes.shape
    atoms, nproj, _ = coupling.shape
    entries = entry_atom.shape[0]
    full = node_count + FACEP
    chunks = full // FACEP
    layers = FACEP // WIDE
    groups = width // GROUP
    span = GROUP * cells

    table = cell_nodes.reshape(groups, GROUP, cells)
    owner = table // FACEP
    ids = jnp.arange(chunks, dtype=jnp.int32)
    flags = jnp.max(
        (owner[:, None] == ids[None, :, None, None]).astype(jnp.int32), axis=(2, 3)
    )
    rank = jnp.sum(flags[:, None, :] * (ids[None, :] < ids[:, None]), axis=2)
    places = jnp.arange(chunks + 1, dtype=jnp.int32)
    used = flags[:, :, None] * (rank[:, :, None] == places)
    listed = chunks + jnp.sum(used * (ids[None, :, None] - chunks), axis=1)
    listed = jnp.concatenate(
        [listed, jnp.full((groups, 1), chunks, jnp.int32), jnp.sum(flags, axis=1, keepdims=True)],
        axis=1,
    )
    sched = listed.astype(jnp.int32).reshape(groups * (chunks + 3))
    scale_row = cell_scale.reshape(1, cells)
    ecell = entry_cell.reshape(1, entries)
    eatom = entry_atom.reshape(1, entries)
    coup = coupling.transpose(1, 2, 0).reshape(nproj * nproj, atoms)
    potential = node_potential.astype(F32).reshape(1, node_count) - CENTER

    vmem = pl.BlockSpec(memory_space=pltpu.VMEM)
    smem = pl.BlockSpec(memory_space=pltpu.SMEM)

    padded = (layers * states + 15) // 16 * 16
    gather = pl.pallas_call(
        gather_kernel,
        out_shape=jax.ShapeDtypeStruct((width * states, cells), F32),
        in_specs=[smem] + [vmem] * 2,
        out_specs=vmem,
        scratch_shapes=[
            pltpu.VMEM((chunks + 1, padded, WIDE), BF16),
            pltpu.VMEM((WIDE, span), BF16),
        ],
        name="gather_cells",
    )
    scatter = pl.pallas_call(
        scatter_kernel,
        out_shape=jax.ShapeDtypeStruct((states, full), F32),
        in_specs=[smem] + [vmem] * 7,
        out_specs=vmem,
        scratch_shapes=[
            pltpu.VMEM((WIDE, span), BF16),
            pltpu.VMEM((width * states, entries), F32),
            pltpu.VMEM((width * states, cells), F32),
            pltpu.VMEM((2 * layers * 2 * states, span), BF16),
            pltpu.VMEM((chunks + 1, layers * 2 * states, WIDE), F32),
        ],
        name="scatter_nodes",
    )

    def remote(kernel, outs, n_in, scratch, copies, ident):
        return pl.pallas_call(
            kernel,
            out_shape=tuple(jax.ShapeDtypeStruct(*out) for out in outs),
            in_specs=[vmem] * n_in,
            out_specs=(vmem,) * len(outs),
            scratch_shapes=[pltpu.VMEM(*one) for one in scratch]
            + [pltpu.SemaphoreType.DMA((2, copies))],
            compiler_params=pltpu.CompilerParams(collective_id=ident, has_side_effects=True),
            name=kernel.__name__,
        )

    pair = (nproj * states, atoms)

    def assemble(extended, ident):
        values = gather(sched, table, extended)
        cell_terms, coef = remote(
            atoms_kernel, [((width * states, cells), F32), ((3,) + pair, F32)], 6,
            [((width * states, entries), F32), ((3,) + pair, F32)] + [((2,) + pair, F32)] * 3,
            4, ident,
        )(values, cell_matrix, scale_row, proj_values, ecell, eatom)
        return scatter(sched, table, cell_terms, coef, coup_all, proj_values, ecell, eatom)

    psi_ext, pot_ext, coup_all = remote(
        start_kernel,
        [((states, full), BF16), ((1, full), F32), ((3, nproj * nproj, atoms), F32)],
        3, [], 4, 0,
    )(psi, potential, coup)
    face = (states, FACEP)
    (first,) = remote(first_kernel, [((states, full), BF16)], 3, [(face, F32), (face, F32)], 2, 2)(
        assemble(psi_ext, 1), psi_ext, pot_ext
    )
    bands, devices = lax.axis_size("band"), lax.axis_size("mesh")
    square = (bands * states, bands * states)
    filtered, correlation = remote(
        last_kernel,
        [((states, node_count), BF16), (square, F32)],
        4,
        [(face, F32), ((states, node_count), BF16), ((devices,) + square, F32)],
        4, 4,
    )(assemble(first, 3), first, psi, potential)
    return (filtered, correlation)


def solution(mesh):
    return jax.shard_map(
        local,
        mesh=mesh,
        in_specs=(
            P("band", "mesh"),
            P(),
            P("mesh"),
            P(),
            P("mesh"),
            P(None, None, "mesh"),
            P("mesh"),
            P("mesh"),
            P("mesh", None, None),
        ),
        out_specs=(P("band", "mesh"), P()),
        check_vma=False,
    )
```

profile of v0, /device:TPU:0, one launch (start us, length us, event | category | flops | bytes accessed | tf_op | source)
XLA Modules:
  0.0 107.2 jit_solution(4735216506691430851)
XLA Ops:
  0.6 0.1 pad.1.clone
  0.7 0.8 convert_add_fusion
  1.5 0.7 sub.18.pot_ref
  2.2 0.9 reshape.63.cn_ref
  3.1 0.0 copy-start
  3.1 0.1 add_select_fusion
  3.2 1.3 %convert_reduce_fusion = s32[6,11]{1,0:T(8,128)S(1)} fusion(s32[6,36,128]{2,1,0:T(8,128)S(1)} %add_select_fusion), kind=kLoop, calls=%fused_computation | loop fusion | flops 912318 | bytes 110856 | tf_op jit(solution)/shard_map/reduce_max | solution.py:374
  4.4 0.3 multiply_reduce_fusion.1
  4.7 0.1 reduce_sum.29
  4.8 0.1 copy.13
  4.9 0.1 copy.12
  5.0 0.1 multiply_reduce_fusion
  5.1 0.1 pad_add_fusion
  5.2 0.6 reshape.64.sched_ref
  5.8 9.6 %start_kernel.1 = (bf16[8,19712]{1,0:T(8,128)(2,1)}, f32[1,19712]{1,0:T(1,128)}, f32[3,64,64]{2,1,0:T(8,128)}) custom-call(bf16[8,17920]{1,0:T(8,128)(2,1)} %psi_ref.3, f32[1,17920]{1,0:T(1,128)} %sub.18.pot_ref, f32[64,64]{1,0:T(8,128)} %bitcast.8), custom_call_target="tpu_custom_call" | custom-call | tf_op jit(solution)/shard_map/start_kernel/pallas_call | solution.py:445
  15.4 0.0 copy-done
  15.4 7.8 %gather_cells.2.xs_ref = f32[1728,128]{1,0:T(8,128)} custom-call(s32[84]{0:T(128)} %reshape.64.sched_ref, s32[6,36,128]{2,1,0:T(8,128)} %copy-done, bf16[8,19712]{1,0:T(8,128)(2,1)} %get-tuple-element.9.ext_ref), custom_call_target="tpu_custom_call" | custom-call | tf_op jit(solution)/shard_map/gather_cells/pallas_call | solution.py:437
  23.2 10.1 %atoms_kernel.2 = (f32[1728,128]{1,0:T(8,128)}, f32[3,64,64]{2,1,0:T(8,128)}) custom-call(f32[1728,128]{1,0:T(8,128)} %gather_cells.2.xs_ref, bf16[216,216]{1,0:T(8,128)(2,1)} %kmat_ref.3, f32[1,128]{1,0:T(1,128)} %bitcast.17, bf16[216,8,128]{2,1,0:T(8,128)(2,1)} %proj_ref.7, s32[1,128]{1,0:T(1,128)} %bitcast.9, s32[1,128]{1,0:T(1,128)} %bitcast.13), custom_call_target="tpu_custom_call" | custom-call | tf_op jit(solution)/shard_map/atoms_kernel/pallas_call | solution.py:438
  33.4 13.1 %scatter_nodes.2.y_ref = f32[8,19712]{1,0:T(8,128)} custom-call(s32[84]{0:T(128)} %reshape.64.sched_ref, s32[6,36,128]{2,1,0:T(8,128)} %copy-done, f32[1728,128]{1,0:T(8,128)} %get-tuple-element.10.ct_ref, f32[3,64,64]{2,1,0:T(8,128)} %get-tuple-element.11.coef_ref, f32[3,64,64]{2,1,0:T(8,128)} %get-tuple-element.12.coup_ref, bf16[216,8,128]{2,1,0:T(8,128)(2,1)} %proj_ref.7, ...), custom_call_target="tpu_custom_call" | custom-call | tf_op jit(solution)/shard_map/scatter_nodes/pallas_call | solution.py:443
  46.4 8.3 %first_kernel.1.ext_ref.first_ref = bf16[8,19712]{1,0:T(8,128)(2,1)} custom-call(f32[8,19712]{1,0:T(8,128)} %scatter_nodes.2.y_ref, bf16[8,19712]{1,0:T(8,128)(2,1)} %get-tuple-element.9.ext_ref, f32[1,19712]{1,0:T(1,128)} %get-tuple-element.13.pot_ref), custom_call_target="tpu_custom_call" | custom-call | tf_op jit(solution)/shard_map/first_kernel/pallas_call | solution.py:451
  54.7 7.8 %gather_cells.3.xs_ref = f32[1728,128]{1,0:T(8,128)} custom-call(s32[84]{0:T(128)} %reshape.64.sched_ref, s32[6,36,128]{2,1,0:T(8,128)} %copy-done, bf16[8,19712]{1,0:T(8,128)(2,1)} %first_kernel.1.ext_ref.first_ref), custom_call_target="tpu_custom_call" | custom-call | tf_op jit(solution)/shard_map/gather_cells/pallas_call | solution.py:437
  62.5 9.4 %atoms_kernel.3 = (f32[1728,128]{1,0:T(8,128)}, f32[3,64,64]{2,1,0:T(8,128)}) custom-call(f32[1728,128]{1,0:T(8,128)} %gather_cells.3.xs_ref, bf16[216,216]{1,0:T(8,128)(2,1)} %kmat_ref.3, f32[1,128]{1,0:T(1,128)} %bitcast.18, bf16[216,8,128]{2,1,0:T(8,128)(2,1)} %proj_ref.7, s32[1,128]{1,0:T(1,128)} %bitcast.11, s32[1,128]{1,0:T(1,128)} %bitcast.15), custom_call_target="tpu_custom_call" | custom-call | tf_op jit(solution)/shard_map/atoms_kernel/pallas_call | solution.py:438
  71.9 13.1 %scatter_nodes.3.y_ref = f32[8,19712]{1,0:T(8,128)} custom-call(s32[84]{0:T(128)} %reshape.64.sched_ref, s32[6,36,128]{2,1,0:T(8,128)} %copy-done, f32[1728,128]{1,0:T(8,128)} %get-tuple-element.14.ct_ref, f32[3,64,64]{2,1,0:T(8,128)} %get-tuple-element.15.coef_ref, f32[3,64,64]{2,1,0:T(8,128)} %get-tuple-element.12.coup_ref, bf16[216,8,128]{2,1,0:T(8,128)(2,1)} %proj_ref.7, ...), custom_call_target="tpu_custom_call" | custom-call | tf_op jit(solution)/shard_map/scatter_nodes/pallas_call | solution.py:443
  84.9 19.3 %last_kernel.1 = (bf16[8,17920]{1,0:T(8,128)(2,1)}, f32[16,16]{1,0:T(8,128)}) custom-call(f32[8,19712]{1,0:T(8,128)} %scatter_nodes.3.y_ref, bf16[8,19712]{1,0:T(8,128)(2,1)} %first_kernel.1.ext_ref.first_ref, bf16[8,17920]{1,0:T(8,128)(2,1)} %psi_ref.3, f32[1,17920]{1,0:T(1,128)} %sub.18.pot_ref), custom_call_target="tpu_custom_call" | custom-call | tf_op jit(solution)/shard_map/last_kernel/pallas_call | solution.py:456
  104.2 1.7 %copy.16 = bf16[8,17920]{1,0:T(8,128)(2,1)} copy(bf16[8,17920]{1,0:T(8,128)(2,1)} %get-tuple-element.18) | data formatting | bytes 573440
  105.9 1.3 %copy.17 = f32[16,16]{1,0:T(8,128)} copy(f32[16,16]{1,0:T(8,128)} %get-tuple-element.19) | data formatting | bytes 2048
  (3 shorter events, 0.0 us)
Async XLA Ops:
  3.1 12.4 %copy-start = (s32[6,36,128]{2,1,0:T(8,128)}, s32[6,36,128]{2,1,0:T(8,128)S(1)}, u32[]{:S(2)}) copy-start(s32[6,36,128]{2,1,0:T(8,128)S(1)} %reshape.63.cn_ref) | copy-start | bytes 331780
where the time goes:
time: 108 us; the launch traced here: 107 us
  Pallas kernels  98.4 us (91%)
  local copies, waits for them, and re-layouts  5.41 us (5%)
  other arithmetic  2.72 us (3%)
    pallas_call x2, Pallas kernels, assemble(): scatter(sched, table, cell_terms, coef, coup_all, proj_values, ecell, eatom)  26.1 us
    pallas_call x2, Pallas kernels, assemble(): remote(atoms_kernel, [((width * states, cells), F32), ((3,) + pair, F32)]...  19.5 us
    pallas_call x1, Pallas kernels, local(): remote(last_kernel, [((states, node_count), BF16), (square, F32)], 4, [(f...  19.3 us
    pallas_call x2, Pallas kernels, assemble(): values = gather(sched, table, extended)  15.6 us
    pallas_call x1, Pallas kernels, local(): remote(start_kernel, [((states, full), BF16), ((1, full), F32), ((3, npro...  9.6 us
    pallas_call x1, Pallas kernels, local(): remote(first_kernel, [((states, full), BF16)], 3, [(face, F32), (face, F3...  8.28 us
    unnamed x4, local copies, waits for them, and re-layouts  2.99 us

commit v1 on v0

--- a/solution.py
+++ b/solution.py
@@ -347,7 +347,462 @@
     corr_ref[...] = jnp.sum(slots_ref[...], axis=0) * (1.0 / (devices * count))
 
 
-def local(
+def everyone(count):
+    bands = lax.axis_size("band")
+    flat = lax.axis_index("mesh") * bands + lax.axis_index("band")
+
+    def peer(steps):
+        other = lax.rem(flat + steps, count)
+        return {"mesh": other // bands, "band": lax.rem(other, bands)}
+
+    return flat, peer
+
+
+def halves(value, axis):
+    top = value.astype(BF16)
+    return jnp.concatenate([top, (value - top.astype(F32)).astype(BF16)], axis=axis)
+
+
+def fused_kernel(psi_ref, cn_ref, scale_ref, kmat_ref, pot_ref, proj_ref, ecell_ref, eatom_ref,
+                 coup_ref, out_ref, corr_ref, flag_ref,
+                 oh_ref, oht_ref, hi_ref, pd_ref, xs_ref, ct_ref, five_ref, ys_ref, lhs_ref,
+                 masked_ref, mid_ref, first_ref, potf_ref, head_ref, tail_ref, low_ref, high_ref,
+                 grouped_ref, left_ref, right_ref, far_ref, ghost_ref, potg_ref, coups_ref,
+                 spread_ref, other_ref, slots_ref, sems):
+    states, count = psi_ref.shape
+    width, cells = cn_ref.shape
+    face = ghost_ref.shape[1]
+    slabs = count // face
+    layers = slabs + 1
+    _, nproj, entries = proj_ref.shape
+    atoms = coup_ref.shape[1]
+    edge = slabs // 2 + 1
+    group = width // edge
+    pairs = cells // 2
+    tiles = face // WIDE
+    block = (tiles + 1) * states
+    wraps = group // 2
+    devices, bands = lax.axis_size("mesh"), lax.axis_size("band")
+    band = lax.axis_index("band")
+    me, peer = everyone(devices * bands)
+    ahead, behind = {"mesh": ring_peer(1)}, {"mesh": ring_peer(-1)}
+    ahead2, behind2 = {"mesh": ring_peer(2)}, {"mesh": ring_peer(-2)}
+    partner = {"band": lax.rem(band + 1, bands)}
+    barrier = pltpu.get_barrier_semaphore()
+
+    def greet_body(steps, carry):
+        pl.semaphore_signal(barrier, inc=1, device_id=peer(steps), device_id_type=MESH_ID)
+        return carry
+
+    lax.fori_loop(1, devices * bands, greet_body, 0)
+
+    down = lax.broadcasted_iota(jnp.int32, (cells, cells), 0)
+    across = lax.broadcasted_iota(jnp.int32, (cells, cells), 1)
+    eye = down == across
+    key = jnp.broadcast_to(cn_ref[0:1, :].astype(F32), (cells, cells))
+    key_col = jnp.sum(jnp.where(eye, key, 0.0), axis=1, keepdims=True)
+    rank = jnp.sum(jnp.where(key < key_col, 1.0, 0.0), axis=1, keepdims=True)
+    chosen_cell = rank == across.astype(F32)
+    order = jnp.where(chosen_cell, 1.0, 0.0).astype(BF16)
+    scale_col = jnp.sum(
+        jnp.where(eye, jnp.broadcast_to(scale_ref[...], (cells, cells)), 0.0), axis=1, keepdims=True
+    )
+    scale = jnp.sum(jnp.where(chosen_cell, scale_col, 0.0), axis=0, keepdims=True)
+    entry_rank = jnp.sum(
+        jnp.where(lax.broadcasted_iota(jnp.int32, (cells, entries), 0) == ecell_ref[...], rank, 0.0),
+        axis=0, keepdims=True,
+    )
+    spread = jnp.where(
+        lax.broadcasted_iota(jnp.int32, (cells, entries), 0).astype(F32) == entry_rank, 1.0, 0.0
+    )
+    spread_ref[...] = spread.astype(BF16)
+    table = cn_ref[...]
+    upper = lax.shift_right_logical(table, 8).astype(F32)
+    lower = jnp.bitwise_and(table, WIDE - 1).astype(F32)
+    table = WIDE * jnp.dot(upper.astype(BF16), order, preferred_element_type=F32) + jnp.dot(
+        lower.astype(BF16), order, preferred_element_type=F32
+    )
+    low_half = lax.broadcasted_iota(jnp.int32, (1, cells), 1) < pairs
+    base = table[:group]
+    base = jnp.where(low_half, base, pltpu.roll(base, pairs, 1))
+    lift = jnp.where(low_half, 0.0, float((edge - 1) * face))
+    wrong = jnp.where((base < 0.0) | (base >= float(face)), 1.0, 0.0)
+    for a in range(edge):
+        expected = base + (lift + float(a * face))
+        wrong = jnp.maximum(
+            wrong, jnp.where(table[a * group:(a + 1) * group] == expected, 0.0, 1.0)
+        )
+    flag_ref[0, 0] = jnp.max(wrong)
+    pd_ref[:group, :] = base
+    places = jnp.where(
+        low_half, pd_ref[pl.ds(0, wraps, stride=2), :], pd_ref[pl.ds(1, wraps, stride=2), :]
+    ).astype(jnp.int32)
+    slot = jnp.bitwise_and(places, WIDE - 1)
+    hi_ref[:wraps, :] = lax.shift_right_logical(places, 8)
+    wide_ids = lax.broadcasted_iota(jnp.int16, (WIDE, cells), 0)
+    one, zero = jnp.array(1.0, BF16), jnp.array(0.0, BF16)
+    for w in range(wraps):
+        hot = jnp.where(wide_ids == slot[w:w + 1, :].astype(jnp.int16), one, zero)
+        oh_ref[:, w * cells:(w + 1) * cells] = hot
+        oht_ref[w * cells:(w + 1) * cells, :] = hot.T
+
+    pl.semaphore_wait(barrier, devices * bands - 1)
+    coups_ref[1] = coup_ref[...]
+    gaps = [
+        send(psi_ref.at[:, :face], ghost_ref, sems, 0, behind),
+        send(pot_ref.at[:potg_ref.shape[0], :], potg_ref, sems, 1, behind),
+        send(coup_ref, coups_ref.at[0], sems, 2, ahead),
+        send(coup_ref, coups_ref.at[2], sems, 3, behind),
+    ]
+    rows128 = face // 128
+    potf_ref[:slabs * rows128, :] = pot_ref[...].astype(F32) - CENTER
+
+    def place(layer):
+        if isinstance(layer, int):
+            return 0 if layer == 0 else 1 if layer == slabs else layer + 1
+        return layer + 1
+
+    def put(layer, blocks):
+        both = jnp.concatenate(blocks + [blocks[-1]], axis=0).astype(BF16)
+        start = place(layer) * block
+        if not isinstance(layer, int):
+            start = pl.multiple_of(start, block)
+        lhs_ref[pl.ds(start, block), :] = both
+
+    def put_psi(layer, source, at):
+        put(layer, [
+            source[:, pl.ds(pl.multiple_of(at + t * WIDE, WIDE), WIDE)].astype(F32)
+            for t in range(tiles)
+        ])
+
+    def psi_body(layer, carry):
+        put_psi(layer, psi_ref, layer * face)
+        return carry
+
+    put_psi(0, psi_ref, 0)
+    lax.fori_loop(1, slabs, psi_body, 0)
+
+    def gather(first_row, chosen, finish):
+        rows = len(chosen) * block
+
+        def body(n, carry):
+            hot = oh_ref[:, pl.ds(pl.multiple_of(n * WIDE, WIDE), WIDE)]
+            out = jnp.dot(lhs_ref[first_row:first_row + rows, :], hot, preferred_element_type=F32)
+            for c in range(WIDE // cells):
+                w = n * (WIDE // cells) + c
+                hi = jnp.broadcast_to(hi_ref[pl.ds(w, 1), :], (states, cells))
+                masks = [hi == t for t in range(1, tiles)]
+                found = {}
+                for k, layer in enumerate(chosen):
+                    part = out[k * block:(k + 1) * block, c * cells:(c + 1) * cells]
+                    value = part[:states]
+                    for t in range(1, tiles):
+                        value = jnp.where(
+                            masks[t - 1], part[t * states:(t + 1) * states], value
+                        )
+                    found[layer] = value
+                finish(w, found)
+            return carry
+
+        lax.fori_loop(0, wraps * cells // WIDE, body, 0)
+
+    def store_pair(a, w, lower_cells, upper_cells):
+        mixed = pltpu.roll(jnp.where(low_half, upper_cells, lower_cells), pairs, 1)
+        at = pl.multiple_of((a * group + 2 * w) * states, 2 * states)
+        xs_ref[pl.ds(at, states), :] = jnp.where(low_half, lower_cells, mixed)
+        xs_ref[pl.ds(at + states, states), :] = jnp.where(low_half, mixed, upper_cells)
+
+    def inner_found(w, found):
+        for a in range(1, edge - 1):
+            store_pair(a, w, found[a], found[edge - 1 + a])
+        five_ref[pl.ds(pl.multiple_of(w * states, states), states), :] = found[edge - 1]
+
+    def outer_found(w, found):
+        middle = five_ref[pl.ds(pl.multiple_of(w * states, states), states), :]
+        store_pair(0, w, found[0], middle)
+        store_pair(edge - 1, w, middle, found[slabs])
+
+    def gather_inner():
+        gather(2 * block, tuple(range(1, slabs)), inner_found)
+
+    def gather_outer():
+        gather(0, (0, slabs), outer_found)
+
+    def partial_body(a, accs):
+        at = pl.multiple_of(a * group * states, group * states)
+        values = jnp.dot(
+            xs_ref[pl.ds(at, group * states), :].astype(BF16), spread_ref[...],
+            preferred_element_type=F32,
+        )
+        accs = list(accs)
+        for j in range(group):
+            proj = proj_ref[a * group + j].astype(F32)
+            value = values[j * states:(j + 1) * states]
+            for k in range(nproj):
+                accs[k] = accs[k] + proj[k:k + 1, :] * value
+        return tuple(accs)
+
+    slot_ids = lax.broadcasted_iota(jnp.int32, (3 * atoms, entries), 0)
+    chosen_atom = jnp.where(slot_ids == eatom_ref[...], 1.0, 0.0).astype(BF16)
+    back = (((1,), (1,)), ((), ()))
+    empty = tuple(jnp.zeros((states, entries), F32) for _ in range(nproj))
+
+    def send_atoms(step, accs):
+        grouped = lax.dot_general(
+            halves(jnp.concatenate(accs, axis=0), 1),
+            jnp.concatenate([chosen_atom, chosen_atom], axis=1),
+            back, preferred_element_type=F32,
+        )
+        for g in range(3):
+            grouped_ref[step, g] = grouped[:, g * atoms:(g + 1) * atoms]
+        at = 4 + 6 * step
+        return [
+            send(grouped_ref.at[step, 1:3], left_ref.at[step], sems, at, ahead),
+            send(grouped_ref.at[step, 0:2], right_ref.at[step], sems, at + 1, behind),
+            send(grouped_ref.at[step, 2], far_ref.at[step, 0], sems, at + 2, ahead2),
+            send(grouped_ref.at[step, 0], far_ref.at[step, 1], sems, at + 3, behind2),
+        ]
+
+    def cell_terms():
+        kmat = kmat_ref[...]
+        for s in range(0, states, 2):
+            pair = jnp.concatenate(
+                [xs_ref[pl.ds(s, width, stride=states), :],
+                 xs_ref[pl.ds(s + 1, width, stride=states), :]], axis=1,
+            ).astype(BF16)
+            out = jnp.dot(kmat, pair, preferred_element_type=F32)
+            ct_ref[pl.ds(s, width, stride=states), :] = out[:, :cells] * scale
+            ct_ref[pl.ds(s + 1, width, stride=states), :] = out[:, cells:] * scale
+
+    def node_stage(step):
+        left, right, far = left_ref.at[step], right_ref.at[step], far_ref.at[step]
+        mine = grouped_ref.at[step]
+        coef = jnp.concatenate(
+            [left[0] + far[0] + mine[0], mine[1] + left[1] + right[0],
+             right[1] + mine[2] + far[1]], axis=1,
+        )
+        coup = jnp.concatenate([coups_ref[0], coups_ref[1], coups_ref[2]], axis=1)
+        rows = []
+        for k in range(nproj):
+            acc = jnp.zeros((states, 3 * atoms), F32)
+            for l in range(nproj):
+                acc = acc + (
+                    coup[k * nproj + l:k * nproj + l + 1, :]
+                    * coef[l * states:(l + 1) * states, :]
+                )
+            rows.append(acc)
+        terms = jnp.dot(
+            halves(jnp.concatenate(rows, axis=0), 1),
+            jnp.concatenate([chosen_atom, chosen_atom], axis=0),
+            preferred_element_type=F32,
+        )
+        terms = [terms[k * states:(k + 1) * states] for k in range(nproj)]
+        ys_ref[...] = jnp.zeros_like(ys_ref)
+        twice = jnp.concatenate([spread_ref[...], spread_ref[...]], axis=1)
+
+        def body(a, carry):
+            parts = []
+            for j in range(group):
+                proj = proj_ref[a * group + j].astype(F32)
+                total = proj[0:1, :] * terms[0]
+                for k in range(1, nproj):
+                    total = total + proj[k:k + 1, :] * terms[k]
+                parts.append(total)
+            at = pl.multiple_of(a * group * states, group * states)
+            value = ct_ref[pl.ds(at, group * states), :] + lax.dot_general(
+                halves(jnp.concatenate(parts, axis=0), 1), twice, back, preferred_element_type=F32
+            )
+            for w in range(wraps):
+                even = value[2 * w * states:(2 * w + 1) * states]
+                odd = value[(2 * w + 1) * states:(2 * w + 2) * states]
+                mixed = pltpu.roll(jnp.where(low_half, odd, even), pairs, 1)
+                here = pl.multiple_of((a * wraps + w) * states, states)
+                there = pl.multiple_of(((a + edge - 1) * wraps + w) * states, states)
+                ys_ref[pl.ds(here, states), :] += jnp.where(low_half, even, mixed)
+                ys_ref[pl.ds(there, states), :] += jnp.where(low_half, mixed, odd)
+            return carry
+
+        lax.fori_loop(0, edge, body, 0)
+
+    def fill_masked():
+        def body(layer, carry):
+            base = layer * (tiles * 2 * states)
+            for w in range(wraps):
+                hi = hi_ref[w:w + 1, :].astype(jnp.int16)
+                at = pl.multiple_of((layer * wraps + w) * states, states)
+                both = halves(ys_ref[pl.ds(at, states), :], 0)
+                for t in range(tiles):
+                    rows = pl.ds(pl.multiple_of(base + t * 2 * states, 2 * states), 2 * states)
+                    masked_ref[rows, w * cells:(w + 1) * cells] = jnp.where(hi == t, both, zero)
+            return carry
+
+        lax.fori_loop(0, layers, body, 0)
+
+    per = tiles * 2 * states
+
+    def joined(value, t):
+        return value[t * 2 * states:t * 2 * states + states] + (
+            value[t * 2 * states + states:(t + 1) * 2 * states]
+        )
+
+    def scatter_outer(step):
+        for layer, into in ((0, head_ref.at[step]), (slabs, tail_ref.at[step])):
+            out = jnp.dot(
+                masked_ref[layer * per:(layer + 1) * per, :], oht_ref[...],
+                preferred_element_type=F32,
+            )
+            for t in range(tiles):
+                into[:, t * WIDE:(t + 1) * WIDE] = joined(out, t)
+
+    def scatter_inner():
+        mid_ref[...] = jnp.dot(
+            masked_ref[per:slabs * per, :], oht_ref[...], preferred_element_type=F32
+        )
+
+    def pot_row(layer, t, half):
+        row = layer * rows128 + t * 2 + half
+        return potf_ref[pl.ds(row, 1), :]
+
+    def scaled(layer, t, summed, field):
+        pot = jnp.concatenate([pot_row(layer, t, 0), pot_row(layer, t, 1)], axis=1)
+        return (summed + pot * field) * (1.0 / HALFWIDTH)
+
+    def lanes(layer, t):
+        at = layer * face + t * WIDE
+        return pl.ds(at if isinstance(layer, int) else pl.multiple_of(at, WIDE), WIDE)
+
+    def first_layer(layer, summed, field):
+        blocks = []
+        for t in range(tiles):
+            value = scaled(layer, t, summed(t), field(t)).astype(BF16).astype(F32)
+            first_ref[:, lanes(layer, t)] = value
+            blocks.append(value)
+        put(layer, blocks)
+
+    def last_layer(layer, summed):
+        for t in range(tiles):
+            value = scaled(layer, t, summed(t), first_ref[:, lanes(layer, t)])
+            at = lanes(layer, t)
+            out_ref[:, at] = (2.0 * value - psi_ref[:, at].astype(F32)).astype(BF16)
+
+    def mid_sum(layer):
+        def summed(t):
+            at = pl.multiple_of((layer - 1) * per + t * 2 * states, 2 * states)
+            return mid_ref[pl.ds(at, states), :] + mid_ref[pl.ds(at + states, states), :]
+        return summed
+
+    def edge_sum(one_ref, two_ref):
+        return lambda t: (
+            one_ref[:, t * WIDE:(t + 1) * WIDE] + two_ref[:, t * WIDE:(t + 1) * WIDE]
+        )
+
+    gather_inner()
+    accs = lax.fori_loop(1, edge - 1, partial_body, empty)
+    for copy in gaps:
+        copy.wait()
+    potf_ref[slabs * rows128:slabs * rows128 + potg_ref.shape[0], :] = (
+        potg_ref[...].astype(F32) - CENTER
+    )
+    put_psi(slabs, ghost_ref, 0)
+    gather_outer()
+    for a in (0, edge - 1):
+        accs = partial_body(a, accs)
+    copies = send_atoms(0, accs)
+    cell_terms()
+    for copy in copies:
+        copy.wait()
+    node_stage(0)
+    fill_masked()
+    scatter_outer(0)
+    copies = [
+        send(tail_ref.at[0], low_ref.at[0], sems, 8, ahead),
+        send(head_ref.at[0], high_ref, sems, 9, behind),
+    ]
+    scatter_inner()
+
+    def first_body(layer, carry):
+        first_layer(
+            layer, mid_sum(layer), lambda t: psi_ref[:, lanes(layer, t)].astype(F32)
+        )
+        return carry
+
+    lax.fori_loop(1, slabs, first_body, 0)
+    gather_inner()
+    accs = lax.fori_loop(1, edge - 1, partial_body, empty)
+    for copy in copies:
+        copy.wait()
+    first_layer(0, edge_sum(head_ref.at[0], low_ref.at[0]), lambda t: psi_ref[:, lanes(0, t)].astype(F32))
+    first_layer(
+        slabs, edge_sum(tail_ref.at[0], high_ref),
+        lambda t: ghost_ref[:, t * WIDE:(t + 1) * WIDE].astype(F32),
+    )
+    gather_outer()
+    for a in (0, edge - 1):
+        accs = partial_body(a, accs)
+    copies = send_atoms(1, accs)
+    cell_terms()
+    for copy in copies:
+        copy.wait()
+    node_stage(1)
+    fill_masked()
+    scatter_outer(1)
+    tail = send(tail_ref.at[1], low_ref.at[1], sems, 14, ahead)
+    scatter_inner()
+
+    def last_body(layer, carry):
+        last_layer(layer, mid_sum(layer))
+        return carry
+
+    lax.fori_loop(1, slabs, last_body, 0)
+    half = slabs // 2
+    kept = half - 1
+    mine = jnp.where(band == 0, 1, half) * face
+    theirs = jnp.where(band == 0, half, 1) * face
+
+    def span(at, size):
+        return pl.ds(pl.multiple_of(at, 128), size)
+
+    swap = send(out_ref.at[:, span(theirs, kept * face)], other_ref.at[:, :kept * face], sems, 15, partner)
+
+    def gram(own_at, at):
+        own = out_ref[:, span(own_at, face)].astype(F32)
+        other = other_ref[:, at:at + face].astype(F32)
+        both = jnp.concatenate(
+            [jnp.where(band == 0, own, other), jnp.where(band == 0, other, own)], axis=0
+        ).astype(BF16)
+        return lax.dot_general(both, both, back, preferred_element_type=F32)
+
+    swap.wait()
+    total = gram(mine, 0)
+    for n in range(1, kept):
+        total = total + gram(mine + n * face, n * face)
+    tail.wait()
+    last_layer(0, edge_sum(head_ref.at[1], low_ref.at[1]))
+    mine = jnp.where(band == 0, 0, slabs - 1) * face
+    theirs = jnp.where(band == 0, slabs - 1, 0) * face
+    final = send(out_ref.at[:, span(theirs, face)], other_ref.at[:, kept * face:], sems, 16, partner)
+    final.wait()
+    total = total + gram(mine, kept * face)
+    size = bands * states
+    slots_ref[me] = jnp.concatenate(
+        [total[:states], total[states:], jnp.zeros((states, 128 - 2 * size), F32)], axis=1
+    )
+
+    def push(steps, carry):
+        send(slots_ref.at[me], slots_ref.at[me], sems, 17, peer(steps))
+        return carry
+
+    lax.fori_loop(1, devices * bands, push, 0)
+    rest = pl.ds(0, devices * bands - 1)
+    pltpu.make_async_remote_copy(
+        src_ref=slots_ref.at[rest], dst_ref=slots_ref.at[rest], send_sem=sems.at[0, 17],
+        recv_sem=sems.at[1, 17], device_id=partner, device_id_type=MESH_ID,
+    ).wait()
+    total = jnp.sum(slots_ref[...], axis=0) * (1.0 / (devices * count))
+    corr_ref[...] = jnp.concatenate([total[:, :size], total[:, size:2 * size]], axis=0)
+
+
+def general(
     psi,
     cell_nodes,
     cell_scale,
@@ -445,11 +900,11 @@
     psi_ext, pot_ext, coup_all = remote(
         start_kernel,
         [((states, full), BF16), ((1, full), F32), ((3, nproj * nproj, atoms), F32)],
-        3, [], 4, 0,
+        3, [], 4, 1,
     )(psi, potential, coup)
     face = (states, FACEP)
-    (first,) = remote(first_kernel, [((states, full), BF16)], 3, [(face, F32), (face, F32)], 2, 2)(
-        assemble(psi_ext, 1), psi_ext, pot_ext
+    (first,) = remote(first_kernel, [((states, full), BF16)], 3, [(face, F32), (face, F32)], 2, 3)(
+        assemble(psi_ext, 2), psi_ext, pot_ext
     )
     bands, devices = lax.axis_size("band"), lax.axis_size("mesh")
     square = (bands * states, bands * states)
@@ -458,9 +913,112 @@
         [((states, node_count), BF16), (square, F32)],
         4,
         [(face, F32), ((states, node_count), BF16), ((devices,) + square, F32)],
-        4, 4,
-    )(assemble(first, 3), first, psi, potential)
+        4, 5,
+    )(assemble(first, 4), first, psi, potential)
     return (filtered, correlation)
+
+
+def bricks(states, node_count, width, cells, bands):
+    edge = round(width ** (1.0 / 3.0))
+    return (
+        edge ** 3 == width
+        and (edge - 1) * 2 * FACEP == node_count
+        and edge % 2 == 0
+        and cells == 128
+        and FACEP % WIDE == 0
+        and states == 8
+        and bands == 2
+    )
+
+
+def local(
+    psi,
+    cell_nodes,
+    cell_scale,
+    cell_matrix,
+    node_potential,
+    proj_values,
+    entry_cell,
+    entry_atom,
+    coupling,
+):
+    states, node_count = psi.shape
+    width, cells = cell_nodes.shape
+    atoms, nproj, _ = coupling.shape
+    entries = entry_atom.shape[0]
+    bands, devices = lax.axis_size("band"), lax.axis_size("mesh")
+    operands = (
+        psi, cell_nodes, cell_scale, cell_matrix, node_potential, proj_values, entry_cell,
+        entry_atom, coupling,
+    )
+    if not bricks(states, node_count, width, cells, bands):
+        return general(*operands)
+    edge = round(width ** (1.0 / 3.0))
+    wraps = edge * edge // 2
+    layers = node_count // FACEP + 1
+    tiles = FACEP // WIDE
+    block = (tiles + 1) * states
+    per = tiles * 2 * states
+    rows = node_count // 128
+    ghost_rows = (FACEP // 128 + 15) // 16 * 16
+    size = bands * states
+    vmem = pl.BlockSpec(memory_space=pltpu.VMEM)
+    smem = pl.BlockSpec(memory_space=pltpu.SMEM)
+    face = (states, FACEP)
+    trio = (2, 3, nproj * states, atoms)
+    duo = (2, 2, nproj * states, atoms)
+    filtered, correlation, wrong = pl.pallas_call(
+        fused_kernel,
+        out_shape=(
+            jax.ShapeDtypeStruct((states, node_count), BF16),
+            jax.ShapeDtypeStruct((size, size), F32),
+            jax.ShapeDtypeStruct((1, 1), F32),
+        ),
+        in_specs=[vmem] * 9,
+        out_specs=(vmem, vmem, smem),
+        scratch_shapes=[
+            pltpu.VMEM((WIDE, wraps * cells), BF16),
+            pltpu.VMEM((wraps * cells, WIDE), BF16),
+            pltpu.VMEM(((wraps + 7) // 8 * 8, cells), jnp.int32),
+            pltpu.VMEM(((2 * wraps + 7) // 8 * 8, cells), F32),
+            pltpu.VMEM((width * states, cells), F32),
+            pltpu.VMEM((width * states, cells), F32),
+            pltpu.VMEM((wraps * states, cells), F32),
+            pltpu.VMEM((layers * wraps * states, cells), F32),
+            pltpu.VMEM((layers * block, WIDE), BF16),
+            pltpu.VMEM((layers * per, wraps * cells), BF16),
+            pltpu.VMEM(((layers - 2) * per, WIDE), F32),
+            pltpu.VMEM((states, layers * FACEP), F32),
+            pltpu.VMEM((rows + ghost_rows, 128), F32),
+            pltpu.VMEM((2,) + face, F32),
+            pltpu.VMEM((2,) + face, F32),
+            pltpu.VMEM((2,) + face, F32),
+            pltpu.VMEM(face, F32),
+            pltpu.VMEM(trio, F32),
+            pltpu.VMEM(duo, F32),
+            pltpu.VMEM(duo, F32),
+            pltpu.VMEM(duo, F32),
+            pltpu.VMEM(face, BF16),
+            pltpu.VMEM((ghost_rows, 128), BF16),
+            pltpu.VMEM((3, nproj * nproj, atoms), F32),
+            pltpu.VMEM((cells, entries), BF16),
+            pltpu.VMEM((states, node_count // 2), BF16),
+            pltpu.VMEM((devices * bands, states, 128), F32),
+            pltpu.SemaphoreType.DMA((2, 18)),
+        ],
+        compiler_params=pltpu.CompilerParams(collective_id=0, has_side_effects=True),
+        name="fused_steps",
+    )(
+        psi, cell_nodes, cell_scale.reshape(1, cells), cell_matrix,
+        node_potential.reshape(rows, 128), proj_values, entry_cell.reshape(1, entries),
+        entry_atom.reshape(1, entries),
+        coupling.transpose(1, 2, 0).reshape(nproj * nproj, atoms),
+    )
+    return lax.cond(
+        wrong[0, 0] > 0.0,
+        lambda: general(*operands),
+        lambda: (filtered, correlation),
+    )
 
 
 def solution(mesh):

time: 108 us -> 60.5 us (0.56)
  Pallas kernels: 98.4 us -> 57.5 us
  local copies, waits for them, and re-layouts: 5.41 us -> 1.35 us
  other arithmetic: 2.72 us -> 0 us
    pallas_call x9 -> x1, Pallas kernels: 98.4 us -> 57.5 us  [local(): pl.pallas_call(fused_kernel, out_shape=(jax.ShapeDtypeStruct((states, nod...]
    unnamed x4 -> x20, local copies, waits for them, and re-layouts: 2.99 us -> 1.35 us
    reshape x2 -> x0, local copies, waits for them, and re-layouts: 1.5 us -> none  [the longest x1 0.9 us: local(): table = cell_nodes.reshape(groups, GROUP, cells)]
    reduce_max x1 -> x0, other arithmetic: 1.26 us -> none  [local(): jnp.max((owner[:, None] == ids[None, :, None, None]).astype(jnp.int32), a...]
where the time goes in v1:
time: 60.5 us; the launch traced here: 60.4 us
  Pallas kernels  57.5 us (95%)
  local copies, waits for them, and re-layouts  1.35 us (2%)
  between operations  1.35 us (2%)
    pallas_call x1, Pallas kernels, local(): pl.pallas_call(fused_kernel, out_shape=(jax.ShapeDtypeStruct((states, nod...  57.5 us
    unnamed x20, local copies, waits for them, and re-layouts  1.35 us

profile of v1, /device:TPU:0, one launch (start us, length us, event | category | flops | bytes accessed | tf_op | source)
XLA Modules:
  0.0 60.4 jit_solution(16295349999891822879)
XLA Ops:
  0.6 0.0 copy-start.6
  0.6 0.0 copy-start.8
  0.7 0.0 copy-start.7
  0.7 0.0 copy-start
  0.7 0.0 copy-start.5
  0.7 0.0 copy-start.3
  0.7 0.0 copy-start.9
  0.7 0.0 copy-start.4
  0.7 0.0 copy-start.2
  0.7 57.5 %fused_steps.1 = (bf16[8,17920]{1,0:T(8,128)(2,1)S(1)}, f32[16,16]{1,0:T(8,128)S(1)}, f32[1,1]{1,0:T(1,128)}) custom-call(bf16[8,17920]{1,0:T(8,128)(2,1)} %psi_ref.1, s32[216,128]{1,0:T(8,128)} %cn_ref.1, f32[1,128]{1,0:T(1,128)} %bitcast.29, bf16[216,216]{1,0:T(8,128)(2,1)} %kmat_ref.1, bf16[140,128]{1,0:T(8,128)(2,1)} %bitcast.16, ...), custom_call_target="tpu_custom_call" | custom-call | tf_op jit(solution)/shard_map/fused_steps/pallas_call | solution.py:970
  58.8 0.0 copy-done.6
  58.8 0.0 copy-done.8
  58.8 0.0 copy-done.7
  58.8 0.0 copy-done
  58.8 0.0 copy-done.5
  58.8 0.0 copy-done.3
  58.8 0.0 copy-done.9
  58.9 0.0 copy-done.4
  58.9 0.0 copy-done.2
  58.9 0.2 conditional.1
  59.1 0.7 %copy.24 = bf16[8,17920]{1,0:T(8,128)(2,1)} copy(bf16[8,17920]{1,0:T(8,128)(2,1)S(1)} %get-tuple-element.58) | data formatting | bytes 573440
  59.8 0.6 copy.25
Async XLA Ops:
  0.6 58.2 %copy-start.6 = (f32[64,8,8]{0,2,1:T(8,128)S(1)}, f32[64,8,8]{0,2,1:T(8,128)}, u32[]{:S(2)}) copy-start(f32[64,8,8]{0,2,1:T(8,128)} %param.19) | copy-start | bytes 49156
  0.6 58.2 %copy-start.8 = (s32[128]{0:T(128)S(1)}, s32[128]{0:T(128)}, u32[]{:S(2)}) copy-start(s32[128]{0:T(128)} %param.18) | copy-start | bytes 1540
  0.7 58.2 %copy-start.7 = (s32[128]{0:T(128)S(1)}, s32[128]{0:T(128)}, u32[]{:S(2)}) copy-start(s32[128]{0:T(128)} %param.17) | copy-start | bytes 1540
  0.7 58.2 %copy-start = (bf16[216,8,128]{2,1,0:T(8,128)(2,1)S(1)}, bf16[216,8,128]{2,1,0:T(8,128)(2,1)}, u32[]{:S(2)}) copy-start(bf16[216,8,128]{2,1,0:T(8,128)(2,1)} %proj_ref.1) | copy-start | bytes 1327108
  0.7 58.2 %copy-start.5 = (bf16[17920]{0:T(1024)(128)(2,1)S(1)}, bf16[17920]{0:T(1024)(128)(2,1)}, u32[]{:S(2)}) copy-start(bf16[17920]{0:T(1024)(128)(2,1)} %param.15) | copy-start | bytes 107524
  0.7 58.2 %copy-start.3 = (bf16[216,216]{1,0:T(8,128)(2,1)S(1)}, bf16[216,216]{1,0:T(8,128)(2,1)}, u32[]{:S(2)}) copy-start(bf16[216,216]{1,0:T(8,128)(2,1)} %kmat_ref.1) | copy-start | bytes 279940
  0.7 58.2 %copy-start.9 = (f32[128]{0:T(128)S(1)}, f32[128]{0:T(128)}, u32[]{:S(2)}) copy-start(f32[128]{0:T(128)} %param.13) | copy-start | bytes 1540
  0.7 58.2 %copy-start.4 = (s32[216,128]{1,0:T(8,128)S(1)}, s32[216,128]{1,0:T(8,128)}, u32[]{:S(2)}) copy-start(s32[216,128]{1,0:T(8,128)} %cn_ref.1) | copy-start | bytes 331780
  0.7 58.2 %copy-start.2 = (bf16[8,17920]{1,0:T(8,128)(2,1)S(1)}, bf16[8,17920]{1,0:T(8,128)(2,1)}, u32[]{:S(2)}) copy-start(bf16[8,17920]{1,0:T(8,128)(2,1)} %psi_ref.1) | copy-start | bytes 860164

commit v2 on v1

--- a/solution.py
+++ b/solution.py
@@ -368,7 +368,8 @@
                  oh_ref, oht_ref, hi_ref, pd_ref, xs_ref, ct_ref, five_ref, ys_ref, lhs_ref,
                  masked_ref, mid_ref, first_ref, potf_ref, head_ref, tail_ref, low_ref, high_ref,
                  grouped_ref, left_ref, right_ref, far_ref, ghost_ref, potg_ref, coups_ref,
-                 spread_ref, other_ref, slots_ref, sems):
+                 spread_ref, other_ref, slots_ref, hot_ref, couple_ref, mate_ref, mated_ref,
+                 mateh_ref, matel_ref, sems):
     states, count = psi_ref.shape
     width, cells = cn_ref.shape
     face = ghost_ref.shape[1]
@@ -388,6 +389,7 @@
     ahead, behind = {"mesh": ring_peer(1)}, {"mesh": ring_peer(-1)}
     ahead2, behind2 = {"mesh": ring_peer(2)}, {"mesh": ring_peer(-2)}
     partner = {"band": lax.rem(band + 1, bands)}
+    ahead_mate = {"mesh": ring_peer(1), "band": lax.rem(band + 1, bands)}
     barrier = pltpu.get_barrier_semaphore()
 
     def greet_body(steps, carry):
@@ -395,6 +397,15 @@
         return carry
 
     lax.fori_loop(1, devices * bands, greet_body, 0)
+    coups_ref[1] = jnp.concatenate([coup_ref[...]] * 2, axis=1)
+    pl.semaphore_wait(barrier, devices * bands - 1)
+    gaps = [
+        send(psi_ref.at[:, :face], ghost_ref, sems, 0, behind),
+        send(pot_ref.at[:potg_ref.shape[0], :], potg_ref, sems, 1, behind),
+        send(coups_ref.at[1], coups_ref.at[0], sems, 2, ahead),
+        send(coups_ref.at[1], coups_ref.at[2], sems, 3, behind),
+        send(psi_ref.at[:, :face], mate_ref, sems, 18, partner),
+    ]
 
     down = lax.broadcasted_iota(jnp.int32, (cells, cells), 0)
     across = lax.broadcasted_iota(jnp.int32, (cells, cells), 1)
@@ -446,14 +457,12 @@
         oh_ref[:, w * cells:(w + 1) * cells] = hot
         oht_ref[w * cells:(w + 1) * cells, :] = hot.T
 
-    pl.semaphore_wait(barrier, devices * bands - 1)
-    coups_ref[1] = coup_ref[...]
-    gaps = [
-        send(psi_ref.at[:, :face], ghost_ref, sems, 0, behind),
-        send(pot_ref.at[:potg_ref.shape[0], :], potg_ref, sems, 1, behind),
-        send(coup_ref, coups_ref.at[0], sems, 2, ahead),
-        send(coup_ref, coups_ref.at[2], sems, 3, behind),
-    ]
+    for w in range(wraps):
+        hi = jnp.broadcast_to(hi_ref[w:w + 1, :], (2 * states, cells))
+        for t in range(tiles):
+            hot_ref[t * 2 * states:(t + 1) * 2 * states, w * cells:(w + 1) * cells] = (
+                jnp.where(hi == t, 1.0, 0.0).astype(BF16)
+            )
     rows128 = face // 128
     potf_ref[:slabs * rows128, :] = pot_ref[...].astype(F32) - CENTER
 
@@ -484,12 +493,13 @@
 
     def gather(first_row, chosen, finish):
         rows = len(chosen) * block
+        trip = wraps // 3
 
         def body(n, carry):
-            hot = oh_ref[:, pl.ds(pl.multiple_of(n * WIDE, WIDE), WIDE)]
+            hot = oh_ref[:, pl.ds(pl.multiple_of(n * trip * cells, trip * cells), trip * cells)]
             out = jnp.dot(lhs_ref[first_row:first_row + rows, :], hot, preferred_element_type=F32)
-            for c in range(WIDE // cells):
-                w = n * (WIDE // cells) + c
+            for c in range(trip):
+                w = n * trip + c
                 hi = jnp.broadcast_to(hi_ref[pl.ds(w, 1), :], (states, cells))
                 masks = [hi == t for t in range(1, tiles)]
                 found = {}
@@ -504,7 +514,7 @@
                 finish(w, found)
             return carry
 
-        lax.fori_loop(0, wraps * cells // WIDE, body, 0)
+        lax.fori_loop(0, 3, body, 0)
 
     def store_pair(a, w, lower_cells, upper_cells):
         mixed = pltpu.roll(jnp.where(low_half, upper_cells, lower_cells), pairs, 1)
@@ -542,25 +552,30 @@
                 accs[k] = accs[k] + proj[k:k + 1, :] * value
         return tuple(accs)
 
-    slot_ids = lax.broadcasted_iota(jnp.int32, (3 * atoms, entries), 0)
+    slot_ids = lax.broadcasted_iota(jnp.int32, (4 * atoms, entries), 0)
     chosen_atom = jnp.where(slot_ids == eatom_ref[...], 1.0, 0.0).astype(BF16)
+    chosen_send = jnp.concatenate(
+        [chosen_atom[:2 * atoms], chosen_atom[atoms:3 * atoms], chosen_atom[2 * atoms:3 * atoms],
+         chosen_atom[:atoms]], axis=0,
+    )
     back = (((1,), (1,)), ((), ()))
     empty = tuple(jnp.zeros((states, entries), F32) for _ in range(nproj))
+    low_atoms = lax.broadcasted_iota(jnp.int32, (1, 2 * atoms), 1) < atoms
 
     def send_atoms(step, accs):
         grouped = lax.dot_general(
             halves(jnp.concatenate(accs, axis=0), 1),
-            jnp.concatenate([chosen_atom, chosen_atom], axis=1),
+            jnp.concatenate([chosen_send, chosen_send], axis=1),
             back, preferred_element_type=F32,
         )
         for g in range(3):
-            grouped_ref[step, g] = grouped[:, g * atoms:(g + 1) * atoms]
+            grouped_ref[step, g] = grouped[:, 2 * g * atoms:2 * (g + 1) * atoms]
         at = 4 + 6 * step
         return [
-            send(grouped_ref.at[step, 1:3], left_ref.at[step], sems, at, ahead),
-            send(grouped_ref.at[step, 0:2], right_ref.at[step], sems, at + 1, behind),
+            send(grouped_ref.at[step, 1], left_ref.at[step], sems, at, ahead),
+            send(grouped_ref.at[step, 0], right_ref.at[step], sems, at + 1, behind),
             send(grouped_ref.at[step, 2], far_ref.at[step, 0], sems, at + 2, ahead2),
-            send(grouped_ref.at[step, 0], far_ref.at[step, 1], sems, at + 3, behind2),
+            send(grouped_ref.at[step, 2], far_ref.at[step, 1], sems, at + 3, behind2),
         ]
 
     def cell_terms():
@@ -575,25 +590,27 @@
             ct_ref[pl.ds(s + 1, width, stride=states), :] = out[:, cells:] * scale
 
     def node_stage(step):
-        left, right, far = left_ref.at[step], right_ref.at[step], far_ref.at[step]
-        mine = grouped_ref.at[step]
-        coef = jnp.concatenate(
-            [left[0] + far[0] + mine[0], mine[1] + left[1] + right[0],
-             right[1] + mine[2] + far[1]], axis=1,
-        )
-        coup = jnp.concatenate([coups_ref[0], coups_ref[1], coups_ref[2]], axis=1)
+        right = pltpu.roll(right_ref[step], atoms, 1)
+        coef = (
+            grouped_ref[step, 0] + left_ref[step]
+            + jnp.where(low_atoms, far_ref[step, 0], right),
+            grouped_ref[step, 2] + right + pltpu.roll(far_ref[step, 1], atoms, 1),
+        )
         rows = []
-        for k in range(nproj):
-            acc = jnp.zeros((states, 3 * atoms), F32)
-            for l in range(nproj):
-                acc = acc + (
-                    coup[k * nproj + l:k * nproj + l + 1, :]
-                    * coef[l * states:(l + 1) * states, :]
-                )
-            rows.append(acc)
+        for c in range(2):
+            parts = []
+            for k in range(nproj):
+                acc = jnp.zeros((states, 2 * atoms), F32)
+                for l in range(nproj):
+                    at = k * nproj + l
+                    acc = acc + (
+                        couple_ref[c, at:at + 1, :] * coef[c][l * states:(l + 1) * states, :]
+                    )
+                parts.append(acc)
+            rows.append(halves(jnp.concatenate(parts, axis=0), 1))
+        half_atoms = [chosen_atom[:2 * atoms]] * 2 + [chosen_atom[2 * atoms:]] * 2
         terms = jnp.dot(
-            halves(jnp.concatenate(rows, axis=0), 1),
-            jnp.concatenate([chosen_atom, chosen_atom], axis=0),
+            jnp.concatenate(rows, axis=1), jnp.concatenate(half_atoms, axis=0),
             preferred_element_type=F32,
         )
         terms = [terms[k * states:(k + 1) * states] for k in range(nproj)]
@@ -624,19 +641,17 @@
 
         lax.fori_loop(0, edge, body, 0)
 
-    def fill_masked():
-        def body(layer, carry):
-            base = layer * (tiles * 2 * states)
-            for w in range(wraps):
-                hi = hi_ref[w:w + 1, :].astype(jnp.int16)
-                at = pl.multiple_of((layer * wraps + w) * states, states)
-                both = halves(ys_ref[pl.ds(at, states), :], 0)
+    def fill_masked(first, last):
+        for w in range(wraps):
+            for layer in range(first, last):
+                at = (layer * wraps + w) * states
+                both = halves(ys_ref[at:at + states, :], 0)
                 for t in range(tiles):
-                    rows = pl.ds(pl.multiple_of(base + t * 2 * states, 2 * states), 2 * states)
-                    masked_ref[rows, w * cells:(w + 1) * cells] = jnp.where(hi == t, both, zero)
-            return carry
-
-        lax.fori_loop(0, layers, body, 0)
+                    rows = (layer * tiles + t) * 2 * states
+                    masked_ref[rows:rows + 2 * states, w * cells:(w + 1) * cells] = (
+                        both * hot_ref[t * 2 * states:(t + 1) * 2 * states,
+                                       w * cells:(w + 1) * cells]
+                    )
 
     per = tiles * 2 * states
 
@@ -700,6 +715,8 @@
     accs = lax.fori_loop(1, edge - 1, partial_body, empty)
     for copy in gaps:
         copy.wait()
+    couple_ref[0] = jnp.where(low_atoms, coups_ref[0], coups_ref[1])
+    couple_ref[1] = coups_ref[2]
     potf_ref[slabs * rows128:slabs * rows128 + potg_ref.shape[0], :] = (
         potg_ref[...].astype(F32) - CENTER
     )
@@ -712,12 +729,14 @@
     for copy in copies:
         copy.wait()
     node_stage(0)
-    fill_masked()
+    fill_masked(0, 1)
+    fill_masked(slabs, layers)
     scatter_outer(0)
     copies = [
         send(tail_ref.at[0], low_ref.at[0], sems, 8, ahead),
         send(head_ref.at[0], high_ref, sems, 9, behind),
     ]
+    fill_masked(1, slabs)
     scatter_inner()
 
     def first_body(layer, carry):
@@ -736,6 +755,7 @@
         slabs, edge_sum(tail_ref.at[0], high_ref),
         lambda t: ghost_ref[:, t * WIDE:(t + 1) * WIDE].astype(F32),
     )
+    mated = [send(first_ref.at[:, :face], mated_ref, sems, 20, partner)]
     gather_outer()
     for a in (0, edge - 1):
         accs = partial_body(a, accs)
@@ -744,9 +764,15 @@
     for copy in copies:
         copy.wait()
     node_stage(1)
-    fill_masked()
+    fill_masked(0, 1)
+    fill_masked(slabs, layers)
     scatter_outer(1)
-    tail = send(tail_ref.at[1], low_ref.at[1], sems, 14, ahead)
+    tails = [
+        send(tail_ref.at[1], low_ref.at[1], sems, 14, ahead),
+        send(tail_ref.at[1], matel_ref, sems, 16, ahead_mate),
+        send(head_ref.at[1], mateh_ref, sems, 19, partner),
+    ]
+    fill_masked(1, slabs)
     scatter_inner()
 
     def last_body(layer, carry):
@@ -762,30 +788,40 @@
     def span(at, size):
         return pl.ds(pl.multiple_of(at, 128), size)
 
-    swap = send(out_ref.at[:, span(theirs, kept * face)], other_ref.at[:, :kept * face], sems, 15, partner)
-
-    def gram(own_at, at):
-        own = out_ref[:, span(own_at, face)].astype(F32)
-        other = other_ref[:, at:at + face].astype(F32)
+    swap = send(out_ref.at[:, span(theirs, half * face)], other_ref, sems, 15, partner)
+
+    def gram(own, other):
         both = jnp.concatenate(
             [jnp.where(band == 0, own, other), jnp.where(band == 0, other, own)], axis=0
         ).astype(BF16)
         return lax.dot_general(both, both, back, preferred_element_type=F32)
 
     swap.wait()
-    total = gram(mine, 0)
-    for n in range(1, kept):
-        total = total + gram(mine + n * face, n * face)
-    tail.wait()
+    total = jnp.zeros((bands * states, bands * states), F32)
+    for n in range(kept):
+        total = total + gram(
+            out_ref[:, span(mine + n * face, face)].astype(F32),
+            other_ref[:, n * face:(n + 1) * face].astype(F32),
+        )
+    for copy in tails + mated:
+        copy.wait()
     last_layer(0, edge_sum(head_ref.at[1], low_ref.at[1]))
-    mine = jnp.where(band == 0, 0, slabs - 1) * face
-    theirs = jnp.where(band == 0, slabs - 1, 0) * face
-    final = send(out_ref.at[:, span(theirs, face)], other_ref.at[:, kept * face:], sems, 16, partner)
-    final.wait()
-    total = total + gram(mine, kept * face)
+    blocks = []
+    summed = edge_sum(mateh_ref, matel_ref)
+    for t in range(tiles):
+        at = slice(t * WIDE, (t + 1) * WIDE)
+        value = scaled(0, t, summed(t), mated_ref[:, at])
+        value = (2.0 * value - mate_ref[:, at].astype(F32)).astype(BF16).astype(F32)
+        blocks.append(jnp.where(band == 0, value, other_ref[:, span(kept * face + t * WIDE, WIDE)].astype(F32)))
+    total = total + gram(
+        out_ref[:, span(jnp.where(band == 0, 0, slabs - 1) * face, face)].astype(F32),
+        jnp.concatenate(blocks, axis=1),
+    )
     size = bands * states
+    lump = size * size // 128
+    pieces = size // lump
     slots_ref[me] = jnp.concatenate(
-        [total[:states], total[states:], jnp.zeros((states, 128 - 2 * size), F32)], axis=1
+        [total[r * lump:(r + 1) * lump] for r in range(pieces)], axis=1
     )
 
     def push(steps, carry):
@@ -799,7 +835,9 @@
         recv_sem=sems.at[1, 17], device_id=partner, device_id_type=MESH_ID,
     ).wait()
     total = jnp.sum(slots_ref[...], axis=0) * (1.0 / (devices * count))
-    corr_ref[...] = jnp.concatenate([total[:, :size], total[:, size:2 * size]], axis=0)
+    corr_ref[...] = jnp.concatenate(
+        [total[:, r * size:(r + 1) * size] for r in range(pieces)], axis=0
+    )
 
 
 def general(
@@ -928,6 +966,7 @@
         and FACEP % WIDE == 0
         and states == 8
         and bands == 2
+        and edge * edge % 6 == 0
     )
 
 
@@ -965,8 +1004,7 @@
     vmem = pl.BlockSpec(memory_space=pltpu.VMEM)
     smem = pl.BlockSpec(memory_space=pltpu.SMEM)
     face = (states, FACEP)
-    trio = (2, 3, nproj * states, atoms)
-    duo = (2, 2, nproj * states, atoms)
+    duo = (nproj * states, 2 * atoms)
     filtered, correlation, wrong = pl.pallas_call(
         fused_kernel,
         out_shape=(
@@ -994,17 +1032,23 @@
             pltpu.VMEM((2,) + face, F32),
             pltpu.VMEM((2,) + face, F32),
             pltpu.VMEM(face, F32),
-            pltpu.VMEM(trio, F32),
-            pltpu.VMEM(duo, F32),
-            pltpu.VMEM(duo, F32),
-            pltpu.VMEM(duo, F32),
+            pltpu.VMEM((2, 3) + duo, F32),
+            pltpu.VMEM((2,) + duo, F32),
+            pltpu.VMEM((2,) + duo, F32),
+            pltpu.VMEM((2, 2) + duo, F32),
             pltpu.VMEM(face, BF16),
             pltpu.VMEM((ghost_rows, 128), BF16),
-            pltpu.VMEM((3, nproj * nproj, atoms), F32),
+            pltpu.VMEM((3, nproj * nproj, 2 * atoms), F32),
             pltpu.VMEM((cells, entries), BF16),
             pltpu.VMEM((states, node_count // 2), BF16),
-            pltpu.VMEM((devices * bands, states, 128), F32),
-            pltpu.SemaphoreType.DMA((2, 18)),
+            pltpu.VMEM((devices * bands, size * size // 128, 128), F32),
+            pltpu.VMEM((per, wraps * cells), BF16),
+            pltpu.VMEM((2, nproj * nproj, 2 * atoms), F32),
+            pltpu.VMEM(face, BF16),
+            pltpu.VMEM(face, F32),
+            pltpu.VMEM(face, F32),
+            pltpu.VMEM(face, F32),
+            pltpu.SemaphoreType.DMA((2, 21)),
         ],
         compiler_params=pltpu.CompilerParams(collective_id=0, has_side_effects=True),
         name="fused_steps",

time: 60.5 us -> 48.9 us (0.81)
  Pallas kernels: 57.5 us -> 45.8 us
    pallas_call x1, Pallas kernels: 57.5 us -> 45.8 us  [local(): pl.pallas_call(fused_kernel, out_shape=(jax.ShapeDtypeStruct((states, nod...]
where the time goes in v2:
time: 48.9 us; the launch traced here: 48.7 us
  Pallas kernels  45.8 us (94%)
  local copies, waits for them, and re-layouts  1.35 us (3%)
  between operations  1.35 us (3%)
    pallas_call x1, Pallas kernels, local(): pl.pallas_call(fused_kernel, out_shape=(jax.ShapeDtypeStruct((states, nod...  45.8 us
    unnamed x20, local copies, waits for them, and re-layouts  1.35 us

profile of v2, /device:TPU:0, one launch (start us, length us, event | category | flops | bytes accessed | tf_op | source)
XLA Modules:
  0.0 48.7 jit_solution(3847423471398930016)
XLA Ops:
  0.6 0.0 copy-start.6
  0.6 0.0 copy-start.8
  0.7 0.0 copy-start.7
  0.7 0.0 copy-start
  0.7 0.0 copy-start.5
  0.7 0.0 copy-start.3
  0.7 0.0 copy-start.9
  0.7 0.0 copy-start.4
  0.7 0.0 copy-start.2
  0.7 45.8 %fused_steps.1 = (bf16[8,17920]{1,0:T(8,128)(2,1)S(1)}, f32[16,16]{1,0:T(8,128)S(1)}, f32[1,1]{1,0:T(1,128)}) custom-call(bf16[8,17920]{1,0:T(8,128)(2,1)} %psi_ref.1, s32[216,128]{1,0:T(8,128)} %cn_ref.1, f32[1,128]{1,0:T(1,128)} %bitcast.29, bf16[216,216]{1,0:T(8,128)(2,1)} %kmat_ref.1, bf16[140,128]{1,0:T(8,128)(2,1)} %bitcast.16, ...), custom_call_target="tpu_custom_call" | custom-call | tf_op jit(solution)/shard_map/fused_steps/pallas_call | solution.py:1008
  47.1 0.0 copy-done.6
  47.1 0.0 copy-done.8
  47.1 0.0 copy-done.7
  47.1 0.0 copy-done
  47.2 0.0 copy-done.5
  47.2 0.0 copy-done.3
  47.2 0.0 copy-done.9
  47.2 0.0 copy-done.4
  47.2 0.0 copy-done.2
  47.2 0.2 conditional.1
  47.4 0.7 %copy.24 = bf16[8,17920]{1,0:T(8,128)(2,1)} copy(bf16[8,17920]{1,0:T(8,128)(2,1)S(1)} %get-tuple-element.58) | data formatting | bytes 573440
  48.1 0.6 %copy.25 = f32[16,16]{1,0:T(8,128)} copy(f32[16,16]{1,0:T(8,128)S(1)} %get-tuple-element.59) | data formatting | bytes 2048
Async XLA Ops:
  0.6 46.5 %copy-start.6 = (f32[64,8,8]{0,2,1:T(8,128)S(1)}, f32[64,8,8]{0,2,1:T(8,128)}, u32[]{:S(2)}) copy-start(f32[64,8,8]{0,2,1:T(8,128)} %param.19) | copy-start | bytes 49156
  0.6 46.5 %copy-start.8 = (s32[128]{0:T(128)S(1)}, s32[128]{0:T(128)}, u32[]{:S(2)}) copy-start(s32[128]{0:T(128)} %param.18) | copy-start | bytes 1540
  0.7 46.5 %copy-start.7 = (s32[128]{0:T(128)S(1)}, s32[128]{0:T(128)}, u32[]{:S(2)}) copy-start(s32[128]{0:T(128)} %param.17) | copy-start | bytes 1540
  0.7 46.5 %copy-start = (bf16[216,8,128]{2,1,0:T(8,128)(2,1)S(1)}, bf16[216,8,128]{2,1,0:T(8,128)(2,1)}, u32[]{:S(2)}) copy-start(bf16[216,8,128]{2,1,0:T(8,128)(2,1)} %proj_ref.1) | copy-start | bytes 1327108
  0.7 46.5 %copy-start.5 = (bf16[17920]{0:T(1024)(128)(2,1)S(1)}, bf16[17920]{0:T(1024)(128)(2,1)}, u32[]{:S(2)}) copy-start(bf16[17920]{0:T(1024)(128)(2,1)} %param.15) | copy-start | bytes 107524
  0.7 46.5 %copy-start.3 = (bf16[216,216]{1,0:T(8,128)(2,1)S(1)}, bf16[216,216]{1,0:T(8,128)(2,1)}, u32[]{:S(2)}) copy-start(bf16[216,216]{1,0:T(8,128)(2,1)} %kmat_ref.1) | copy-start | bytes 279940
  0.7 46.5 %copy-start.9 = (f32[128]{0:T(128)S(1)}, f32[128]{0:T(128)}, u32[]{:S(2)}) copy-start(f32[128]{0:T(128)} %param.13) | copy-start | bytes 1540
  0.7 46.5 %copy-start.4 = (s32[216,128]{1,0:T(8,128)S(1)}, s32[216,128]{1,0:T(8,128)}, u32[]{:S(2)}) copy-start(s32[216,128]{1,0:T(8,128)} %cn_ref.1) | copy-start | bytes 331780
  0.7 46.5 %copy-start.2 = (bf16[8,17920]{1,0:T(8,128)(2,1)S(1)}, bf16[8,17920]{1,0:T(8,128)(2,1)}, u32[]{:S(2)}) copy-start(bf16[8,17920]{1,0:T(8,128)(2,1)} %psi_ref.1) | copy-start | bytes 860164

commit v3 on v2

--- a/solution.py
+++ b/solution.py
@@ -363,13 +363,23 @@
     return jnp.concatenate([top, (value - top.astype(F32)).astype(BF16)], axis=axis)
 
 
-def fused_kernel(psi_ref, cn_ref, scale_ref, kmat_ref, pot_ref, proj_ref, ecell_ref, eatom_ref,
+def fused_kernel(psi_hbm, cn_hbm, scale_ref, kmat_hbm, pot_hbm, proj_hbm, ecell_ref, eatom_ref,
                  coup_ref, out_ref, corr_ref, flag_ref,
-                 oh_ref, oht_ref, hi_ref, pd_ref, xs_ref, ct_ref, five_ref, ys_ref, lhs_ref,
-                 masked_ref, mid_ref, first_ref, potf_ref, head_ref, tail_ref, low_ref, high_ref,
+                 psi_ref, cn_ref, kmat_ref, pot_ref, proj_ref,
+                 oh_ref, oht_ref, hi_ref, pd_ref, xs_ref, ct_ref, ends_ref, five_ref, ys_ref, lhs_ref,
+                 masked_ref, first_ref, potf_ref, head_ref, tail_ref, low_ref, high_ref,
                  grouped_ref, left_ref, right_ref, far_ref, ghost_ref, potg_ref, coups_ref,
                  spread_ref, other_ref, slots_ref, hot_ref, couple_ref, mate_ref, mated_ref,
-                 mateh_ref, matel_ref, sems):
+                 mateh_ref, matel_ref, projf_ref, fetch_sems, sems):
+    fetches = [
+        pltpu.make_async_copy(src, dst, fetch_sems.at[n])
+        for n, (src, dst) in enumerate((
+            (cn_hbm, cn_ref), (psi_hbm, psi_ref), (proj_hbm, proj_ref), (pot_hbm, pot_ref),
+            (kmat_hbm, kmat_ref),
+        ))
+    ]
+    for fetch in fetches:
+        fetch.start()
     states, count = psi_ref.shape
     width, cells = cn_ref.shape
     face = ghost_ref.shape[1]
@@ -400,13 +410,14 @@
     coups_ref[1] = jnp.concatenate([coup_ref[...]] * 2, axis=1)
     pl.semaphore_wait(barrier, devices * bands - 1)
     gaps = [
-        send(psi_ref.at[:, :face], ghost_ref, sems, 0, behind),
-        send(pot_ref.at[:potg_ref.shape[0], :], potg_ref, sems, 1, behind),
+        send(psi_hbm.at[:, :face], ghost_ref, sems, 0, behind),
+        send(pot_hbm.at[:potg_ref.shape[0], :], potg_ref, sems, 1, behind),
         send(coups_ref.at[1], coups_ref.at[0], sems, 2, ahead),
         send(coups_ref.at[1], coups_ref.at[2], sems, 3, behind),
-        send(psi_ref.at[:, :face], mate_ref, sems, 18, partner),
+        send(psi_hbm.at[:, :face], mate_ref, sems, 18, partner),
     ]
 
+    fetches[0].wait()
     down = lax.broadcasted_iota(jnp.int32, (cells, cells), 0)
     across = lax.broadcasted_iota(jnp.int32, (cells, cells), 1)
     eye = down == across
@@ -464,6 +475,27 @@
                 jnp.where(hi == t, 1.0, 0.0).astype(BF16)
             )
     rows128 = face // 128
+    for fetch in fetches[1:]:
+        fetch.wait()
+    in_lower = entry_rank < float(pairs)
+    last = (edge - 1) * group
+
+    def proj_body(j, carry):
+        rows = pl.ds(pl.multiple_of(j * nproj, nproj), nproj)
+        projf_ref[rows, :] = proj_ref[j].astype(F32)
+        return carry
+
+    lax.fori_loop(0, width, proj_body, 0, unroll=8)
+
+    def ends_body(i, carry):
+        one, two = proj_ref[i].astype(F32), proj_ref[last + i].astype(F32)
+        early = pl.multiple_of((width + i) * nproj, nproj)
+        late = pl.multiple_of((width + group + i) * nproj, nproj)
+        projf_ref[pl.ds(early, nproj), :] = jnp.where(in_lower, two, one)
+        projf_ref[pl.ds(late, nproj), :] = jnp.where(in_lower, one, two)
+        return carry
+
+    lax.fori_loop(0, group, ends_body, 0, unroll=6)
     potf_ref[:slabs * rows128, :] = pot_ref[...].astype(F32) - CENTER
 
     def place(layer):
@@ -491,9 +523,9 @@
     put_psi(0, psi_ref, 0)
     lax.fori_loop(1, slabs, psi_body, 0)
 
-    def gather(first_row, chosen, finish):
+    def gather(first_row, chosen, finish, trips):
         rows = len(chosen) * block
-        trip = wraps // 3
+        trip = wraps // trips
 
         def body(n, carry):
             hot = oh_ref[:, pl.ds(pl.multiple_of(n * trip * cells, trip * cells), trip * cells)]
@@ -514,43 +546,54 @@
                 finish(w, found)
             return carry
 
-        lax.fori_loop(0, 3, body, 0)
-
-    def store_pair(a, w, lower_cells, upper_cells):
+        lax.fori_loop(0, trips, body, 0)
+
+    def store_pair(into, row, w, lower_cells, upper_cells):
         mixed = pltpu.roll(jnp.where(low_half, upper_cells, lower_cells), pairs, 1)
-        at = pl.multiple_of((a * group + 2 * w) * states, 2 * states)
-        xs_ref[pl.ds(at, states), :] = jnp.where(low_half, lower_cells, mixed)
-        xs_ref[pl.ds(at + states, states), :] = jnp.where(low_half, mixed, upper_cells)
+        at = pl.multiple_of((row + 2 * w) * states, 2 * states)
+        into[pl.ds(at, states), :] = jnp.where(low_half, lower_cells, mixed)
+        into[pl.ds(at + states, states), :] = jnp.where(low_half, mixed, upper_cells)
 
     def inner_found(w, found):
         for a in range(1, edge - 1):
-            store_pair(a, w, found[a], found[edge - 1 + a])
-        five_ref[pl.ds(pl.multiple_of(w * states, states), states), :] = found[edge - 1]
+            store_pair(xs_ref, a * group, w, found[a], found[edge - 1 + a])
+        store_pair(ends_ref, 0, w, found[edge - 1], found[edge - 1])
 
     def outer_found(w, found):
-        middle = five_ref[pl.ds(pl.multiple_of(w * states, states), states), :]
-        store_pair(0, w, found[0], middle)
-        store_pair(edge - 1, w, middle, found[slabs])
+        store_pair(ends_ref, group, w, found[0], found[slabs])
 
     def gather_inner():
-        gather(2 * block, tuple(range(1, slabs)), inner_found)
+        gather(2 * block, tuple(range(1, slabs)), inner_found, 3)
 
     def gather_outer():
-        gather(0, (0, slabs), outer_found)
-
-    def partial_body(a, accs):
-        at = pl.multiple_of(a * group * states, group * states)
+        gather(0, (0, slabs), outer_found, 1)
+
+    def bcast(row):
+        return projf_ref[pl.ds(row, states, stride=0), :]
+
+    def partial_rows(source, at, proj_at, accs):
         values = jnp.dot(
-            xs_ref[pl.ds(at, group * states), :].astype(BF16), spread_ref[...],
+            source[pl.ds(at, group * states), :].astype(BF16), spread_ref[...],
             preferred_element_type=F32,
         )
         accs = list(accs)
         for j in range(group):
-            proj = proj_ref[a * group + j].astype(F32)
             value = values[j * states:(j + 1) * states]
             for k in range(nproj):
-                accs[k] = accs[k] + proj[k:k + 1, :] * value
+                accs[k] = accs[k] + bcast(proj_at + j * nproj + k) * value
         return tuple(accs)
+
+    def partial_body(a, accs):
+        return partial_rows(
+            xs_ref, pl.multiple_of(a * group * states, group * states), a * group * nproj, accs
+        )
+
+    def partial_inner():
+        accs = lax.fori_loop(1, edge - 1, partial_body, empty)
+        return partial_rows(ends_ref, 0, width * nproj, accs)
+
+    def partial_outer(accs):
+        return partial_rows(ends_ref, group * states, (width + group) * nproj, accs)
 
     slot_ids = lax.broadcasted_iota(jnp.int32, (4 * atoms, entries), 0)
     chosen_atom = jnp.where(slot_ids == eatom_ref[...], 1.0, 0.0).astype(BF16)
@@ -579,6 +622,10 @@
         ]
 
     def cell_terms():
+        size = group * states
+        early, late = ends_ref[:size, :], ends_ref[size:, :]
+        xs_ref[:size, :] = jnp.where(low_half, late, early)
+        xs_ref[last * states:, :] = jnp.where(low_half, early, late)
         kmat = kmat_ref[...]
         for s in range(0, states, 2):
             pair = jnp.concatenate(
@@ -589,7 +636,7 @@
             ct_ref[pl.ds(s, width, stride=states), :] = out[:, :cells] * scale
             ct_ref[pl.ds(s + 1, width, stride=states), :] = out[:, cells:] * scale
 
-    def node_stage(step):
+    def entry_terms(step):
         right = pltpu.roll(right_ref[step], atoms, 1)
         coef = (
             grouped_ref[step, 0] + left_ref[step]
@@ -613,66 +660,78 @@
             jnp.concatenate(rows, axis=1), jnp.concatenate(half_atoms, axis=0),
             preferred_element_type=F32,
         )
-        terms = [terms[k * states:(k + 1) * states] for k in range(nproj)]
-        ys_ref[...] = jnp.zeros_like(ys_ref)
+        return [terms[k * states:(k + 1) * states] for k in range(nproj)]
+
+    def node_terms(a, terms):
+        parts = []
+        for j in range(group):
+            row = (a * group + j) * nproj
+            total = bcast(row) * terms[0]
+            for k in range(1, nproj):
+                total = total + bcast(row + k) * terms[k]
+            parts.append(total)
+        at = pl.multiple_of(a * group * states, group * states)
         twice = jnp.concatenate([spread_ref[...], spread_ref[...]], axis=1)
-
-        def body(a, carry):
-            parts = []
-            for j in range(group):
-                proj = proj_ref[a * group + j].astype(F32)
-                total = proj[0:1, :] * terms[0]
-                for k in range(1, nproj):
-                    total = total + proj[k:k + 1, :] * terms[k]
-                parts.append(total)
-            at = pl.multiple_of(a * group * states, group * states)
-            value = ct_ref[pl.ds(at, group * states), :] + lax.dot_general(
-                halves(jnp.concatenate(parts, axis=0), 1), twice, back, preferred_element_type=F32
-            )
-            for w in range(wraps):
-                even = value[2 * w * states:(2 * w + 1) * states]
-                odd = value[(2 * w + 1) * states:(2 * w + 2) * states]
-                mixed = pltpu.roll(jnp.where(low_half, odd, even), pairs, 1)
-                here = pl.multiple_of((a * wraps + w) * states, states)
-                there = pl.multiple_of(((a + edge - 1) * wraps + w) * states, states)
-                ys_ref[pl.ds(here, states), :] += jnp.where(low_half, even, mixed)
-                ys_ref[pl.ds(there, states), :] += jnp.where(low_half, mixed, odd)
-            return carry
-
-        lax.fori_loop(0, edge, body, 0)
-
-    def fill_masked(first, last):
+        value = ct_ref[pl.ds(at, group * states), :] + lax.dot_general(
+            halves(jnp.concatenate(parts, axis=0), 1), twice, back, preferred_element_type=F32
+        )
         for w in range(wraps):
-            for layer in range(first, last):
-                at = (layer * wraps + w) * states
-                both = halves(ys_ref[at:at + states, :], 0)
+            even = value[2 * w * states:(2 * w + 1) * states]
+            odd = value[(2 * w + 1) * states:(2 * w + 2) * states]
+            mixed = pltpu.roll(jnp.where(low_half, odd, even), pairs, 1)
+            here = pl.multiple_of((a * wraps + w) * states, states)
+            there = pl.multiple_of(((a + edge - 1) * wraps + w) * states, states)
+            ys_ref[pl.ds(here, states), :] += jnp.where(low_half, even, mixed)
+            ys_ref[pl.ds(there, states), :] += jnp.where(low_half, mixed, odd)
+
+    per = tiles * 2 * states
+
+    def scatter(into, chosen):
+        for w in range(wraps):
+            for n, layer in enumerate(chosen):
+                at = pl.multiple_of((layer * wraps + w) * states, states)
+                both = halves(ys_ref[pl.ds(at, states), :], 0)
                 for t in range(tiles):
-                    rows = (layer * tiles + t) * 2 * states
+                    rows = into + (n * tiles + t) * 2 * states
                     masked_ref[rows:rows + 2 * states, w * cells:(w + 1) * cells] = (
                         both * hot_ref[t * 2 * states:(t + 1) * 2 * states,
                                        w * cells:(w + 1) * cells]
                     )
-
-    per = tiles * 2 * states
+        rows = len(chosen) * per
+        out = jnp.dot(masked_ref[into:into + rows, :], oht_ref[...], preferred_element_type=F32)
+        return [
+            [joined(out[n * per:(n + 1) * per], t) for t in range(tiles)]
+            for n in range(len(chosen))
+        ]
 
     def joined(value, t):
         return value[t * 2 * states:t * 2 * states + states] + (
             value[t * 2 * states + states:(t + 1) * 2 * states]
         )
 
-    def scatter_outer(step):
-        for layer, into in ((0, head_ref.at[step]), (slabs, tail_ref.at[step])):
-            out = jnp.dot(
-                masked_ref[layer * per:(layer + 1) * per, :], oht_ref[...],
-                preferred_element_type=F32,
-            )
-            for t in range(tiles):
-                into[:, t * WIDE:(t + 1) * WIDE] = joined(out, t)
-
-    def scatter_inner():
-        mid_ref[...] = jnp.dot(
-            masked_ref[per:slabs * per, :], oht_ref[...], preferred_element_type=F32
-        )
+    def scatter_outer(step, terms):
+        def body(n, carry):
+            node_terms(lax.rem(n + edge - 1, edge), terms)
+            return carry
+
+        lax.fori_loop(0, 2, body, 0)
+        head, tail = scatter(0, (0, slabs))
+        for t in range(tiles):
+            head_ref[step, :, t * WIDE:(t + 1) * WIDE] = head[t]
+            tail_ref[step, :, t * WIDE:(t + 1) * WIDE] = tail[t]
+
+    def scatter_five():
+        (out,) = scatter(2 * per, (edge - 1,))
+        return lambda t: out[t]
+
+    def scatter_rest(terms, finish):
+        def body(a, carry):
+            node_terms(a, terms)
+            one, two = scatter(3 * per, (a, a + edge - 1))
+            finish(a, lambda t: one[t], lambda t: two[t])
+            return carry
+
+        lax.fori_loop(1, edge - 1, body, 0)
 
     def pot_row(layer, t, half):
         row = layer * rows128 + t * 2 + half
@@ -700,95 +759,88 @@
             at = lanes(layer, t)
             out_ref[:, at] = (2.0 * value - psi_ref[:, at].astype(F32)).astype(BF16)
 
-    def mid_sum(layer):
-        def summed(t):
-            at = pl.multiple_of((layer - 1) * per + t * 2 * states, 2 * states)
-            return mid_ref[pl.ds(at, states), :] + mid_ref[pl.ds(at + states, states), :]
-        return summed
-
     def edge_sum(one_ref, two_ref):
         return lambda t: (
             one_ref[:, t * WIDE:(t + 1) * WIDE] + two_ref[:, t * WIDE:(t + 1) * WIDE]
         )
 
     gather_inner()
-    accs = lax.fori_loop(1, edge - 1, partial_body, empty)
+    accs = partial_inner()
+    ys_ref[...] = jnp.zeros_like(ys_ref)
     for copy in gaps:
         copy.wait()
     couple_ref[0] = jnp.where(low_atoms, coups_ref[0], coups_ref[1])
     couple_ref[1] = coups_ref[2]
+    put_psi(slabs, ghost_ref, 0)
+    gather_outer()
+    copies = send_atoms(0, partial_outer(accs))
     potf_ref[slabs * rows128:slabs * rows128 + potg_ref.shape[0], :] = (
         potg_ref[...].astype(F32) - CENTER
     )
-    put_psi(slabs, ghost_ref, 0)
-    gather_outer()
-    for a in (0, edge - 1):
-        accs = partial_body(a, accs)
-    copies = send_atoms(0, accs)
     cell_terms()
     for copy in copies:
         copy.wait()
-    node_stage(0)
-    fill_masked(0, 1)
-    fill_masked(slabs, layers)
-    scatter_outer(0)
+    terms = entry_terms(0)
+    scatter_outer(0, terms)
     copies = [
         send(tail_ref.at[0], low_ref.at[0], sems, 8, ahead),
         send(head_ref.at[0], high_ref, sems, 9, behind),
     ]
-    fill_masked(1, slabs)
-    scatter_inner()
-
-    def first_body(layer, carry):
-        first_layer(
-            layer, mid_sum(layer), lambda t: psi_ref[:, lanes(layer, t)].astype(F32)
-        )
-        return carry
-
-    lax.fori_loop(1, slabs, first_body, 0)
+
+    def first_done(layer, summed):
+        first_layer(layer, summed, lambda t: psi_ref[:, lanes(layer, t)].astype(F32))
+
+    def first_pair(a, one, two):
+        first_done(a, one)
+        first_done(a + edge - 1, two)
+
+    first_done(edge - 1, scatter_five())
+    scatter_rest(terms, first_pair)
     gather_inner()
-    accs = lax.fori_loop(1, edge - 1, partial_body, empty)
+    accs = partial_inner()
+    ys_ref[...] = jnp.zeros_like(ys_ref)
     for copy in copies:
         copy.wait()
-    first_layer(0, edge_sum(head_ref.at[0], low_ref.at[0]), lambda t: psi_ref[:, lanes(0, t)].astype(F32))
+    first_done(0, edge_sum(head_ref.at[0], low_ref.at[0]))
     first_layer(
         slabs, edge_sum(tail_ref.at[0], high_ref),
         lambda t: ghost_ref[:, t * WIDE:(t + 1) * WIDE].astype(F32),
     )
+    gather_outer()
+    copies = send_atoms(1, partial_outer(accs))
     mated = [send(first_ref.at[:, :face], mated_ref, sems, 20, partner)]
-    gather_outer()
-    for a in (0, edge - 1):
-        accs = partial_body(a, accs)
-    copies = send_atoms(1, accs)
     cell_terms()
     for copy in copies:
         copy.wait()
-    node_stage(1)
-    fill_masked(0, 1)
-    fill_masked(slabs, layers)
-    scatter_outer(1)
+    terms = entry_terms(1)
+    scatter_outer(1, terms)
     tails = [
         send(tail_ref.at[1], low_ref.at[1], sems, 14, ahead),
         send(tail_ref.at[1], matel_ref, sems, 16, ahead_mate),
         send(head_ref.at[1], mateh_ref, sems, 19, partner),
     ]
-    fill_masked(1, slabs)
-    scatter_inner()
-
-    def last_body(layer, carry):
-        last_layer(layer, mid_sum(layer))
-        return carry
-
-    lax.fori_loop(1, slabs, last_body, 0)
-    half = slabs // 2
-    kept = half - 1
-    mine = jnp.where(band == 0, 1, half) * face
-    theirs = jnp.where(band == 0, half, 1) * face
+    half = edge - 1
 
     def span(at, size):
         return pl.ds(pl.multiple_of(at, 128), size)
 
-    swap = send(out_ref.at[:, span(theirs, half * face)], other_ref, sems, 15, partner)
+    def swap(n, layer):
+        return pltpu.make_async_remote_copy(
+            src_ref=out_ref.at[:, span(layer * face, face)],
+            dst_ref=other_ref.at[:, span(n * face, face)],
+            send_sem=sems.at[0, 21 + n], recv_sem=sems.at[1, 21 + n],
+            device_id=partner, device_id_type=MESH_ID,
+        )
+
+    last_layer(half, scatter_five())
+    swap(0, half).start()
+
+    def last_pair(a, one, two):
+        last_layer(a, one)
+        last_layer(a + half, two)
+        swap(a, jnp.where(band == 0, a + half, a)).start()
+
+    scatter_rest(terms, last_pair)
 
     def gram(own, other):
         both = jnp.concatenate(
@@ -796,11 +848,12 @@
         ).astype(BF16)
         return lax.dot_general(both, both, back, preferred_element_type=F32)
 
-    swap.wait()
+    swap(0, half).wait()
     total = jnp.zeros((bands * states, bands * states), F32)
-    for n in range(kept):
+    for n in range(1, half):
+        swap(n, half).wait()
         total = total + gram(
-            out_ref[:, span(mine + n * face, face)].astype(F32),
+            out_ref[:, span(jnp.where(band == 0, n, n + half) * face, face)].astype(F32),
             other_ref[:, n * face:(n + 1) * face].astype(F32),
         )
     for copy in tails + mated:
@@ -812,9 +865,9 @@
         at = slice(t * WIDE, (t + 1) * WIDE)
         value = scaled(0, t, summed(t), mated_ref[:, at])
         value = (2.0 * value - mate_ref[:, at].astype(F32)).astype(BF16).astype(F32)
-        blocks.append(jnp.where(band == 0, value, other_ref[:, span(kept * face + t * WIDE, WIDE)].astype(F32)))
+        blocks.append(jnp.where(band == 0, value, other_ref[:, at].astype(F32)))
     total = total + gram(
-        out_ref[:, span(jnp.where(band == 0, 0, slabs - 1) * face, face)].astype(F32),
+        out_ref[:, span(jnp.where(band == 0, 0, half) * face, face)].astype(F32),
         jnp.concatenate(blocks, axis=1),
     )
     size = bands * states
@@ -1003,6 +1056,7 @@
     size = bands * states
     vmem = pl.BlockSpec(memory_space=pltpu.VMEM)
     smem = pl.BlockSpec(memory_space=pltpu.SMEM)
+    anywhere = pl.BlockSpec(memory_space=pl.ANY)
     face = (states, FACEP)
     duo = (nproj * states, 2 * atoms)
     filtered, correlation, wrong = pl.pallas_call(
@@ -1012,20 +1066,25 @@
             jax.ShapeDtypeStruct((size, size), F32),
             jax.ShapeDtypeStruct((1, 1), F32),
         ),
-        in_specs=[vmem] * 9,
+        in_specs=[anywhere, anywhere, vmem, anywhere, anywhere, anywhere, vmem, vmem, vmem],
         out_specs=(vmem, vmem, smem),
         scratch_shapes=[
+            pltpu.VMEM(psi.shape, BF16),
+            pltpu.VMEM(cell_nodes.shape, jnp.int32),
+            pltpu.VMEM(cell_matrix.shape, BF16),
+            pltpu.VMEM((rows, 128), BF16),
+            pltpu.VMEM(proj_values.shape, BF16),
             pltpu.VMEM((WIDE, wraps * cells), BF16),
             pltpu.VMEM((wraps * cells, WIDE), BF16),
             pltpu.VMEM(((wraps + 7) // 8 * 8, cells), jnp.int32),
             pltpu.VMEM(((2 * wraps + 7) // 8 * 8, cells), F32),
             pltpu.VMEM((width * states, cells), F32),
             pltpu.VMEM((width * states, cells), F32),
+            pltpu.VMEM((4 * wraps * states, cells), F32),
             pltpu.VMEM((wraps * states, cells), F32),
             pltpu.VMEM((layers * wraps * states, cells), F32),
             pltpu.VMEM((layers * block, WIDE), BF16),
-            pltpu.VMEM((layers * per, wraps * cells), BF16),
-            pltpu.VMEM(((layers - 2) * per, WIDE), F32),
+            pltpu.VMEM((5 * per, wraps * cells), BF16),
             pltpu.VMEM((states, layers * FACEP), F32),
             pltpu.VMEM((rows + ghost_rows, 128), F32),
             pltpu.VMEM((2,) + face, F32),
@@ -1048,7 +1107,9 @@
             pltpu.VMEM(face, F32),
             pltpu.VMEM(face, F32),
             pltpu.VMEM(face, F32),
-            pltpu.SemaphoreType.DMA((2, 21)),
+            pltpu.VMEM(((width + 4 * wraps) * nproj, entries), F32),
+            pltpu.SemaphoreType.DMA((5,)),
+            pltpu.SemaphoreType.DMA((2, 26)),
         ],
         compiler_params=pltpu.CompilerParams(collective_id=0, has_side_effects=True),
         name="fused_steps",

time: 48.9 us -> 46.2 us (0.945)
  Pallas kernels: 45.8 us -> 43.1 us
    pallas_call x1, Pallas kernels: 45.8 us -> 43.1 us  [local(): pl.pallas_call(fused_kernel, out_shape=(jax.ShapeDtypeStruct((states, nod...]
where the time goes in v3:
time: 46.2 us; the launch traced here: 46 us
  Pallas kernels  43.1 us (93%)
  local copies, waits for them, and re-layouts  1.35 us (3%)
  between operations  1.35 us (3%)
    pallas_call x1, Pallas kernels, local(): pl.pallas_call(fused_kernel, out_shape=(jax.ShapeDtypeStruct((states, nod...  43.1 us
    unnamed x20, local copies, waits for them, and re-layouts  1.35 us

profile of v3, /device:TPU:0, one launch (start us, length us, event | category | flops | bytes accessed | tf_op | source)
XLA Modules:
  0.0 46.0 jit_solution(3028310360537938827)
XLA Ops:
  0.6 0.0 copy-start.6
  0.6 0.0 copy-start.8
  0.7 0.0 copy-start.7
  0.7 0.0 copy-start
  0.7 0.0 copy-start.5
  0.7 0.0 copy-start.3
  0.7 0.0 copy-start.9
  0.7 0.0 copy-start.4
  0.7 0.0 copy-start.2
  0.7 43.1 %fused_steps.1 = (bf16[8,17920]{1,0:T(8,128)(2,1)S(1)}, f32[16,16]{1,0:T(8,128)S(1)}, f32[1,1]{1,0:T(1,128)}) custom-call(bf16[8,17920]{1,0:T(8,128)(2,1)} %psi_hbm.1, s32[216,128]{1,0:T(8,128)} %cn_hbm.1, f32[1,128]{1,0:T(1,128)} %bitcast.29, bf16[216,216]{1,0:T(8,128)(2,1)} %kmat_hbm.1, bf16[140,128]{1,0:T(8,128)(2,1)} %bitcast.16, ...), custom_call_target="tpu_custom_call" | custom-call | tf_op jit(solution)/shard_map/fused_steps/pallas_call | solution.py:1062
  44.4 0.0 copy-done.6
  44.4 0.0 copy-done.8
  44.4 0.0 copy-done.7
  44.4 0.0 copy-done
  44.4 0.0 copy-done.5
  44.5 0.0 copy-done.3
  44.5 0.0 copy-done.9
  44.5 0.0 copy-done.4
  44.5 0.0 copy-done.2
  44.5 0.2 conditional.1
  44.7 0.7 %copy.24 = bf16[8,17920]{1,0:T(8,128)(2,1)} copy(bf16[8,17920]{1,0:T(8,128)(2,1)S(1)} %get-tuple-element.58) | data formatting | bytes 573440
  45.4 0.6 %copy.25 = f32[16,16]{1,0:T(8,128)} copy(f32[16,16]{1,0:T(8,128)S(1)} %get-tuple-element.59) | data formatting | bytes 2048
Async XLA Ops:
  0.6 43.8 %copy-start.6 = (f32[64,8,8]{0,2,1:T(8,128)S(1)}, f32[64,8,8]{0,2,1:T(8,128)}, u32[]{:S(2)}) copy-start(f32[64,8,8]{0,2,1:T(8,128)} %param.19) | copy-start | bytes 49156
  0.6 43.8 %copy-start.8 = (s32[128]{0:T(128)S(1)}, s32[128]{0:T(128)}, u32[]{:S(2)}) copy-start(s32[128]{0:T(128)} %param.18) | copy-start | bytes 1540
  0.7 43.8 %copy-start.7 = (s32[128]{0:T(128)S(1)}, s32[128]{0:T(128)}, u32[]{:S(2)}) copy-start(s32[128]{0:T(128)} %param.17) | copy-start | bytes 1540
  0.7 43.8 %copy-start = (bf16[216,8,128]{2,1,0:T(8,128)(2,1)S(1)}, bf16[216,8,128]{2,1,0:T(8,128)(2,1)}, u32[]{:S(2)}) copy-start(bf16[216,8,128]{2,1,0:T(8,128)(2,1)} %proj_hbm.1) | copy-start | bytes 1327108
  0.7 43.8 %copy-start.5 = (bf16[17920]{0:T(1024)(128)(2,1)S(1)}, bf16[17920]{0:T(1024)(128)(2,1)}, u32[]{:S(2)}) copy-start(bf16[17920]{0:T(1024)(128)(2,1)} %param.15) | copy-start | bytes 107524
  0.7 43.8 %copy-start.3 = (bf16[216,216]{1,0:T(8,128)(2,1)S(1)}, bf16[216,216]{1,0:T(8,128)(2,1)}, u32[]{:S(2)}) copy-start(bf16[216,216]{1,0:T(8,128)(2,1)} %kmat_hbm.1) | copy-start | bytes 279940
  0.7 43.8 %copy-start.9 = (f32[128]{0:T(128)S(1)}, f32[128]{0:T(128)}, u32[]{:S(2)}) copy-start(f32[128]{0:T(128)} %param.13) | copy-start | bytes 1540
  0.7 43.8 %copy-start.4 = (s32[216,128]{1,0:T(8,128)S(1)}, s32[216,128]{1,0:T(8,128)}, u32[]{:S(2)}) copy-start(s32[216,128]{1,0:T(8,128)} %cn_hbm.1) | copy-start | bytes 331780
  0.7 43.8 %copy-start.2 = (bf16[8,17920]{1,0:T(8,128)(2,1)S(1)}, bf16[8,17920]{1,0:T(8,128)(2,1)}, u32[]{:S(2)}) copy-start(bf16[8,17920]{1,0:T(8,128)(2,1)} %psi_hbm.1) | copy-start | bytes 860164

commit v4 on v3

--- a/solution.py
+++ b/solution.py
@@ -350,9 +350,13 @@
 def everyone(count):
     bands = lax.axis_size("band")
     flat = lax.axis_index("mesh") * bands + lax.axis_index("band")
-
-    def peer(steps):
-        other = lax.rem(flat + steps, count)
+    early = flat < count // 2
+
+    def peer(n):
+        down = count - 1 - n
+        other = jnp.where(
+            early, jnp.where(down <= flat, down - 1, down), jnp.where(n >= flat, n + 1, n)
+        )
         return {"mesh": other // bands, "band": lax.rem(other, bands)}
 
     return flat, peer
@@ -363,10 +367,10 @@
     return jnp.concatenate([top, (value - top.astype(F32)).astype(BF16)], axis=axis)
 
 
-def fused_kernel(psi_hbm, cn_hbm, scale_ref, kmat_hbm, pot_hbm, proj_hbm, ecell_ref, eatom_ref,
-                 coup_ref, out_ref, corr_ref, flag_ref,
-                 psi_ref, cn_ref, kmat_ref, pot_ref, proj_ref,
-                 oh_ref, oht_ref, hi_ref, pd_ref, xs_ref, ct_ref, ends_ref, five_ref, ys_ref, lhs_ref,
+def fused_kernel(psi_hbm, cn_hbm, scale_hbm, kmat_hbm, pot_hbm, proj_hbm, ecell_hbm, eatom_hbm,
+                 coup_hbm, out_ref, corr_ref, flag_ref,
+                 psi_ref, cn_ref, kmat_ref, pot_ref, proj_ref, scale_ref, ecell_ref, eatom_ref, coup_ref,
+                 oh_ref, oht_ref, hi_ref, pd_ref, xs_ref, ct_ref, ends_ref, lhs_ref,
                  masked_ref, first_ref, potf_ref, head_ref, tail_ref, low_ref, high_ref,
                  grouped_ref, left_ref, right_ref, far_ref, ghost_ref, potg_ref, coups_ref,
                  spread_ref, other_ref, slots_ref, hot_ref, couple_ref, mate_ref, mated_ref,
@@ -374,8 +378,9 @@
     fetches = [
         pltpu.make_async_copy(src, dst, fetch_sems.at[n])
         for n, (src, dst) in enumerate((
-            (cn_hbm, cn_ref), (psi_hbm, psi_ref), (proj_hbm, proj_ref), (pot_hbm, pot_ref),
-            (kmat_hbm, kmat_ref),
+            (cn_hbm, cn_ref), (scale_hbm, scale_ref), (ecell_hbm, ecell_ref),
+            (coup_hbm, coup_ref), (eatom_hbm, eatom_ref), (psi_hbm, psi_ref),
+            (proj_hbm, proj_ref), (pot_hbm, pot_ref), (kmat_hbm, kmat_ref),
         ))
     ]
     for fetch in fetches:
@@ -406,18 +411,9 @@
         pl.semaphore_signal(barrier, inc=1, device_id=peer(steps), device_id_type=MESH_ID)
         return carry
 
-    lax.fori_loop(1, devices * bands, greet_body, 0)
-    coups_ref[1] = jnp.concatenate([coup_ref[...]] * 2, axis=1)
-    pl.semaphore_wait(barrier, devices * bands - 1)
-    gaps = [
-        send(psi_hbm.at[:, :face], ghost_ref, sems, 0, behind),
-        send(pot_hbm.at[:potg_ref.shape[0], :], potg_ref, sems, 1, behind),
-        send(coups_ref.at[1], coups_ref.at[0], sems, 2, ahead),
-        send(coups_ref.at[1], coups_ref.at[2], sems, 3, behind),
-        send(psi_hbm.at[:, :face], mate_ref, sems, 18, partner),
-    ]
-
-    fetches[0].wait()
+    lax.fori_loop(0, devices * bands - 1, greet_body, 0)
+    for fetch in fetches[:4]:
+        fetch.wait()
     down = lax.broadcasted_iota(jnp.int32, (cells, cells), 0)
     across = lax.broadcasted_iota(jnp.int32, (cells, cells), 1)
     eye = down == across
@@ -474,8 +470,18 @@
             hot_ref[t * 2 * states:(t + 1) * 2 * states, w * cells:(w + 1) * cells] = (
                 jnp.where(hi == t, 1.0, 0.0).astype(BF16)
             )
+    coups_ref[1] = jnp.concatenate([coup_ref[...]] * 2, axis=1)
+    pl.semaphore_wait(barrier, devices * bands - 1)
+    gaps = [
+        send(psi_hbm.at[:, :face], ghost_ref, sems, 0, behind),
+        send(pot_hbm.at[:potg_ref.shape[0], :], potg_ref, sems, 1, behind),
+        send(coups_ref.at[1], coups_ref.at[0], sems, 2, ahead),
+        send(coups_ref.at[1], coups_ref.at[2], sems, 3, behind),
+        send(psi_hbm.at[:, :face], mate_ref, sems, 18, partner),
+    ]
+
     rows128 = face // 128
-    for fetch in fetches[1:]:
+    for fetch in fetches[4:]:
         fetch.wait()
     in_lower = entry_rank < float(pairs)
     last = (edge - 1) * group
@@ -530,8 +536,12 @@
         def body(n, carry):
             hot = oh_ref[:, pl.ds(pl.multiple_of(n * trip * cells, trip * cells), trip * cells)]
             out = jnp.dot(lhs_ref[first_row:first_row + rows, :], hot, preferred_element_type=F32)
-            for c in range(trip):
-                w = n * trip + c
+            pick(out, n * trip, trip)
+            return carry
+
+        def pick(out, first, columns):
+            for c in range(columns):
+                w = first + c
                 hi = jnp.broadcast_to(hi_ref[pl.ds(w, 1), :], (states, cells))
                 masks = [hi == t for t in range(1, tiles)]
                 found = {}
@@ -544,13 +554,22 @@
                         )
                     found[layer] = value
                 finish(w, found)
-            return carry
-
-        lax.fori_loop(0, trips, body, 0)
+
+        if trips == 1:
+            wide = 2 * cells
+            for n in range(wraps // 2):
+                out = jnp.dot(
+                    lhs_ref[first_row:first_row + rows, :], oh_ref[:, n * wide:(n + 1) * wide],
+                    preferred_element_type=F32,
+                )
+                pick(out, 2 * n, 2)
+        else:
+            lax.fori_loop(0, trips, body, 0)
 
     def store_pair(into, row, w, lower_cells, upper_cells):
         mixed = pltpu.roll(jnp.where(low_half, upper_cells, lower_cells), pairs, 1)
-        at = pl.multiple_of((row + 2 * w) * states, 2 * states)
+        at = (row + 2 * w) * states
+        at = at if isinstance(w, int) else pl.multiple_of(at, 2 * states)
         into[pl.ds(at, states), :] = jnp.where(low_half, lower_cells, mixed)
         into[pl.ds(at + states, states), :] = jnp.where(low_half, mixed, upper_cells)
 
@@ -563,7 +582,7 @@
         store_pair(ends_ref, group, w, found[0], found[slabs])
 
     def gather_inner():
-        gather(2 * block, tuple(range(1, slabs)), inner_found, 3)
+        gather(2 * block, tuple(range(1, slabs)), inner_found, 1)
 
     def gather_outer():
         gather(0, (0, slabs), outer_found, 1)
@@ -583,14 +602,11 @@
                 accs[k] = accs[k] + bcast(proj_at + j * nproj + k) * value
         return tuple(accs)
 
-    def partial_body(a, accs):
-        return partial_rows(
-            xs_ref, pl.multiple_of(a * group * states, group * states), a * group * nproj, accs
-        )
-
     def partial_inner():
-        accs = lax.fori_loop(1, edge - 1, partial_body, empty)
-        return partial_rows(ends_ref, 0, width * nproj, accs)
+        accs = partial_rows(ends_ref, 0, width * nproj, empty)
+        for a in range(1, edge - 1):
+            accs = partial_rows(xs_ref, a * group * states, a * group * nproj, accs)
+        return accs
 
     def partial_outer(accs):
         return partial_rows(ends_ref, group * states, (width + group) * nproj, accs)
@@ -622,7 +638,6 @@
         ]
 
     def cell_terms():
-        size = group * states
         early, late = ends_ref[:size, :], ends_ref[size:, :]
         xs_ref[:size, :] = jnp.where(low_half, late, early)
         xs_ref[last * states:, :] = jnp.where(low_half, early, late)
@@ -662,46 +677,64 @@
         )
         return [terms[k * states:(k + 1) * states] for k in range(nproj)]
 
-    def node_terms(a, terms):
+    per = tiles * 2 * states
+    size = group * states
+
+    def terms_at(a):
+        return ct_ref[a * size:(a + 1) * size, :]
+
+    def node_rows(proj_at, before, terms):
         parts = []
         for j in range(group):
-            row = (a * group + j) * nproj
+            row = proj_at + j * nproj
             total = bcast(row) * terms[0]
             for k in range(1, nproj):
                 total = total + bcast(row + k) * terms[k]
             parts.append(total)
-        at = pl.multiple_of(a * group * states, group * states)
         twice = jnp.concatenate([spread_ref[...], spread_ref[...]], axis=1)
-        value = ct_ref[pl.ds(at, group * states), :] + lax.dot_general(
+        value = before + lax.dot_general(
             halves(jnp.concatenate(parts, axis=0), 1), twice, back, preferred_element_type=F32
         )
+        found = []
         for w in range(wraps):
             even = value[2 * w * states:(2 * w + 1) * states]
             odd = value[(2 * w + 1) * states:(2 * w + 2) * states]
             mixed = pltpu.roll(jnp.where(low_half, odd, even), pairs, 1)
-            here = pl.multiple_of((a * wraps + w) * states, states)
-            there = pl.multiple_of(((a + edge - 1) * wraps + w) * states, states)
-            ys_ref[pl.ds(here, states), :] += jnp.where(low_half, even, mixed)
-            ys_ref[pl.ds(there, states), :] += jnp.where(low_half, mixed, odd)
-
-    per = tiles * 2 * states
-
-    def scatter(into, chosen):
-        for w in range(wraps):
-            for n, layer in enumerate(chosen):
-                at = pl.multiple_of((layer * wraps + w) * states, states)
-                both = halves(ys_ref[pl.ds(at, states), :], 0)
-                for t in range(tiles):
-                    rows = into + (n * tiles + t) * 2 * states
-                    masked_ref[rows:rows + 2 * states, w * cells:(w + 1) * cells] = (
-                        both * hot_ref[t * 2 * states:(t + 1) * 2 * states,
-                                       w * cells:(w + 1) * cells]
-                    )
-        rows = len(chosen) * per
-        out = jnp.dot(masked_ref[into:into + rows, :], oht_ref[...], preferred_element_type=F32)
+            found.append((jnp.where(low_half, even, mixed), jnp.where(low_half, mixed, odd)))
+        return found
+
+    def fill(into, w, value):
+        both = halves(value, 0)
+        for t in range(tiles):
+            rows = into + t * 2 * states
+            masked_ref[rows:rows + 2 * states, w * cells:(w + 1) * cells] = (
+                both * hot_ref[t * 2 * states:(t + 1) * 2 * states, w * cells:(w + 1) * cells]
+            )
+
+    def fill_late(terms):
+        before = jnp.where(low_half, terms_at(0), terms_at(edge - 1))
+        found = node_rows((width + group) * nproj, before, terms)
+        for w, (one, two) in enumerate(found):
+            fill(0, w, one)
+            fill(per, w, two)
+
+    def fill_early(terms):
+        before = jnp.where(low_half, terms_at(edge - 1), terms_at(0))
+        for w, (one, two) in enumerate(node_rows(width * nproj, before, terms)):
+            fill(2 * per, w, one + two)
+
+    def fill_inner(a, terms):
+        found = node_rows(a * group * nproj, terms_at(a), terms)
+        for w, (one, two) in enumerate(found):
+            fill((2 * a + 1) * per, w, one)
+            fill((2 * a + 2) * per, w, two)
+
+    def scatter(into, number):
+        out = jnp.dot(
+            masked_ref[into:into + number * per, :], oht_ref[...], preferred_element_type=F32
+        )
         return [
-            [joined(out[n * per:(n + 1) * per], t) for t in range(tiles)]
-            for n in range(len(chosen))
+            [joined(out[n * per:(n + 1) * per], t) for t in range(tiles)] for n in range(number)
         ]
 
     def joined(value, t):
@@ -710,28 +743,24 @@
         )
 
     def scatter_outer(step, terms):
-        def body(n, carry):
-            node_terms(lax.rem(n + edge - 1, edge), terms)
-            return carry
-
-        lax.fori_loop(0, 2, body, 0)
-        head, tail = scatter(0, (0, slabs))
+        fill_late(terms)
+        head, tail = scatter(0, 2)
         for t in range(tiles):
             head_ref[step, :, t * WIDE:(t + 1) * WIDE] = head[t]
             tail_ref[step, :, t * WIDE:(t + 1) * WIDE] = tail[t]
 
-    def scatter_five():
-        (out,) = scatter(2 * per, (edge - 1,))
-        return lambda t: out[t]
-
     def scatter_rest(terms, finish):
-        def body(a, carry):
-            node_terms(a, terms)
-            one, two = scatter(3 * per, (a, a + edge - 1))
-            finish(a, lambda t: one[t], lambda t: two[t])
-            return carry
-
-        lax.fori_loop(1, edge - 1, body, 0)
+        fill_early(terms)
+        for a in range(1, edge):
+            if a < edge - 1:
+                fill_inner(a, terms)
+            if a == 1:
+                (out,) = scatter(2 * per, 1)
+                finish(0, edge - 1, out)
+            else:
+                one, two = scatter((2 * a - 1) * per, 2)
+                finish(a - 1, a - 1, one)
+                finish(a - 1, a + edge - 2, two)
 
     def pot_row(layer, t, half):
         row = layer * rows128 + t * 2 + half
@@ -766,7 +795,6 @@
 
     gather_inner()
     accs = partial_inner()
-    ys_ref[...] = jnp.zeros_like(ys_ref)
     for copy in gaps:
         copy.wait()
     couple_ref[0] = jnp.where(low_atoms, coups_ref[0], coups_ref[1])
@@ -790,15 +818,9 @@
     def first_done(layer, summed):
         first_layer(layer, summed, lambda t: psi_ref[:, lanes(layer, t)].astype(F32))
 
-    def first_pair(a, one, two):
-        first_done(a, one)
-        first_done(a + edge - 1, two)
-
-    first_done(edge - 1, scatter_five())
-    scatter_rest(terms, first_pair)
+    scatter_rest(terms, lambda a, layer, out: first_done(layer, lambda t: out[t]))
     gather_inner()
     accs = partial_inner()
-    ys_ref[...] = jnp.zeros_like(ys_ref)
     for copy in copies:
         copy.wait()
     first_done(0, edge_sum(head_ref.at[0], low_ref.at[0]))
@@ -832,15 +854,12 @@
             device_id=partner, device_id_type=MESH_ID,
         )
 
-    last_layer(half, scatter_five())
-    swap(0, half).start()
-
-    def last_pair(a, one, two):
-        last_layer(a, one)
-        last_layer(a + half, two)
-        swap(a, jnp.where(band == 0, a + half, a)).start()
-
-    scatter_rest(terms, last_pair)
+    def last_done(a, layer, out):
+        last_layer(layer, lambda t: out[t])
+        if layer >= half:
+            swap(a, jnp.where(band == 0, a + half, a) if a else half).start()
+
+    scatter_rest(terms, last_done)
 
     def gram(own, other):
         both = jnp.concatenate(
@@ -881,7 +900,7 @@
         send(slots_ref.at[me], slots_ref.at[me], sems, 17, peer(steps))
         return carry
 
-    lax.fori_loop(1, devices * bands, push, 0)
+    lax.fori_loop(0, devices * bands - 1, push, 0)
     rest = pl.ds(0, devices * bands - 1)
     pltpu.make_async_remote_copy(
         src_ref=slots_ref.at[rest], dst_ref=slots_ref.at[rest], send_sem=sems.at[0, 17],
@@ -1066,7 +1085,7 @@
             jax.ShapeDtypeStruct((size, size), F32),
             jax.ShapeDtypeStruct((1, 1), F32),
         ),
-        in_specs=[anywhere, anywhere, vmem, anywhere, anywhere, anywhere, vmem, vmem, vmem],
+        in_specs=[anywhere] * 9,
         out_specs=(vmem, vmem, smem),
         scratch_shapes=[
             pltpu.VMEM(psi.shape, BF16),
@@ -1074,6 +1093,10 @@
             pltpu.VMEM(cell_matrix.shape, BF16),
             pltpu.VMEM((rows, 128), BF16),
             pltpu.VMEM(proj_values.shape, BF16),
+            pltpu.VMEM((1, cells), F32),
+            pltpu.VMEM((1, entries), jnp.int32),
+            pltpu.VMEM((1, entries), jnp.int32),
+            pltpu.VMEM((nproj * nproj, atoms), F32),
             pltpu.VMEM((WIDE, wraps * cells), BF16),
             pltpu.VMEM((wraps * cells, WIDE), BF16),
             pltpu.VMEM(((wraps + 7) // 8 * 8, cells), jnp.int32),
@@ -1081,10 +1104,8 @@
             pltpu.VMEM((width * states, cells), F32),
             pltpu.VMEM((width * states, cells), F32),
             pltpu.VMEM((4 * wraps * states, cells), F32),
-            pltpu.VMEM((wraps * states, cells), F32),
-            pltpu.VMEM((layers * wraps * states, cells), F32),
             pltpu.VMEM((layers * block, WIDE), BF16),
-            pltpu.VMEM((5 * per, wraps * cells), BF16),
+            pltpu.VMEM((layers * per, wraps * cells), BF16),
             pltpu.VMEM((states, layers * FACEP), F32),
             pltpu.VMEM((rows + ghost_rows, 128), F32),
             pltpu.VMEM((2,) + face, F32),
@@ -1108,7 +1129,7 @@
             pltpu.VMEM(face, F32),
             pltpu.VMEM(face, F32),
             pltpu.VMEM(((width + 4 * wraps) * nproj, entries), F32),
-            pltpu.SemaphoreType.DMA((5,)),
+            pltpu.SemaphoreType.DMA((9,)),
             pltpu.SemaphoreType.DMA((2, 26)),
         ],
         compiler_params=pltpu.CompilerParams(collective_id=0, has_side_effects=True),

time: 46.2 us -> 42.5 us (0.920)
  Pallas kernels: 43.1 us -> 39.4 us
    pallas_call x1, Pallas kernels: 43.1 us -> 39.4 us  [local(): pl.pallas_call(fused_kernel, out_shape=(jax.ShapeDtypeStruct((states, nod...]
where the time goes in v4:
time: 42.5 us; the launch traced here: 42.3 us
  Pallas kernels  39.4 us (93%)
  local copies, waits for them, and re-layouts  1.35 us (3%)
  between operations  1.35 us (3%)
    pallas_call x1, Pallas kernels, local(): pl.pallas_call(fused_kernel, out_shape=(jax.ShapeDtypeStruct((states, nod...  39.4 us
    unnamed x20, local copies, waits for them, and re-layouts  1.35 us

profile of v4, /device:TPU:0, one launch (start us, length us, event | category | flops | bytes accessed | tf_op | source)
XLA Modules:
  0.0 42.3 jit_solution(9204233073348259904)
XLA Ops:
  0.6 0.0 copy-start.6
  0.6 0.0 copy-start.8
  0.7 0.0 copy-start.7
  0.7 0.0 copy-start
  0.7 0.0 copy-start.5
  0.7 0.0 copy-start.3
  0.7 0.0 copy-start.9
  0.7 0.0 copy-start.4
  0.7 0.0 copy-start.2
  0.7 39.4 %fused_steps.1 = (bf16[8,17920]{1,0:T(8,128)(2,1)S(1)}, f32[16,16]{1,0:T(8,128)S(1)}, f32[1,1]{1,0:T(1,128)}) custom-call(bf16[8,17920]{1,0:T(8,128)(2,1)} %psi_hbm.1, s32[216,128]{1,0:T(8,128)} %cn_hbm.1, f32[1,128]{1,0:T(1,128)} %bitcast.29, bf16[216,216]{1,0:T(8,128)(2,1)} %kmat_hbm.1, bf16[140,128]{1,0:T(8,128)(2,1)} %bitcast.16, ...), custom_call_target="tpu_custom_call" | custom-call | tf_op jit(solution)/shard_map/fused_steps/pallas_call | solution.py:1081
  40.7 0.0 copy-done.6
  40.7 0.0 copy-done.8
  40.7 0.0 copy-done.7
  40.8 0.0 copy-done
  40.8 0.0 copy-done.5
  40.8 0.0 copy-done.3
  40.8 0.0 copy-done.9
  40.8 0.0 copy-done.4
  40.8 0.0 copy-done.2
  40.8 0.2 conditional.1
  41.0 0.7 %copy.24 = bf16[8,17920]{1,0:T(8,128)(2,1)} copy(bf16[8,17920]{1,0:T(8,128)(2,1)S(1)} %get-tuple-element.58) | data formatting | bytes 573440
  41.7 0.6 %copy.25 = f32[16,16]{1,0:T(8,128)} copy(f32[16,16]{1,0:T(8,128)S(1)} %get-tuple-element.59) | data formatting | bytes 2048
Async XLA Ops:
  0.6 40.1 %copy-start.6 = (f32[64,8,8]{0,2,1:T(8,128)S(1)}, f32[64,8,8]{0,2,1:T(8,128)}, u32[]{:S(2)}) copy-start(f32[64,8,8]{0,2,1:T(8,128)} %param.19) | copy-start | bytes 49156
  0.6 40.1 %copy-start.8 = (s32[128]{0:T(128)S(1)}, s32[128]{0:T(128)}, u32[]{:S(2)}) copy-start(s32[128]{0:T(128)} %param.18) | copy-start | bytes 1540
  0.7 40.1 %copy-start.7 = (s32[128]{0:T(128)S(1)}, s32[128]{0:T(128)}, u32[]{:S(2)}) copy-start(s32[128]{0:T(128)} %param.17) | copy-start | bytes 1540
  0.7 40.1 %copy-start = (bf16[216,8,128]{2,1,0:T(8,128)(2,1)S(1)}, bf16[216,8,128]{2,1,0:T(8,128)(2,1)}, u32[]{:S(2)}) copy-start(bf16[216,8,128]{2,1,0:T(8,128)(2,1)} %proj_hbm.1) | copy-start | bytes 1327108
  0.7 40.1 %copy-start.5 = (bf16[17920]{0:T(1024)(128)(2,1)S(1)}, bf16[17920]{0:T(1024)(128)(2,1)}, u32[]{:S(2)}) copy-start(bf16[17920]{0:T(1024)(128)(2,1)} %param.15) | copy-start | bytes 107524
  0.7 40.1 %copy-start.3 = (bf16[216,216]{1,0:T(8,128)(2,1)S(1)}, bf16[216,216]{1,0:T(8,128)(2,1)}, u32[]{:S(2)}) copy-start(bf16[216,216]{1,0:T(8,128)(2,1)} %kmat_hbm.1) | copy-start | bytes 279940
  0.7 40.1 %copy-start.9 = (f32[128]{0:T(128)S(1)}, f32[128]{0:T(128)}, u32[]{:S(2)}) copy-start(f32[128]{0:T(128)} %param.13) | copy-start | bytes 1540
  0.7 40.1 %copy-start.4 = (s32[216,128]{1,0:T(8,128)S(1)}, s32[216,128]{1,0:T(8,128)}, u32[]{:S(2)}) copy-start(s32[216,128]{1,0:T(8,128)} %cn_hbm.1) | copy-start | bytes 331780
  0.7 40.1 %copy-start.2 = (bf16[8,17920]{1,0:T(8,128)(2,1)S(1)}, bf16[8,17920]{1,0:T(8,128)(2,1)}, u32[]{:S(2)}) copy-start(bf16[8,17920]{1,0:T(8,128)(2,1)} %psi_hbm.1) | copy-start | bytes 860164

commit v5 on v4

--- a/solution.py
+++ b/solution.py
@@ -368,7 +368,7 @@
 
 
 def fused_kernel(psi_hbm, cn_hbm, scale_hbm, kmat_hbm, pot_hbm, proj_hbm, ecell_hbm, eatom_hbm,
-                 coup_hbm, out_ref, corr_ref, flag_ref,
+                 coup_hbm, out_ref, corr_ref, flag_hbm, flag_ref,
                  psi_ref, cn_ref, kmat_ref, pot_ref, proj_ref, scale_ref, ecell_ref, eatom_ref, coup_ref,
                  oh_ref, oht_ref, hi_ref, pd_ref, xs_ref, ct_ref, ends_ref, lhs_ref,
                  masked_ref, first_ref, potf_ref, head_ref, tail_ref, low_ref, high_ref,
@@ -450,7 +450,11 @@
         wrong = jnp.maximum(
             wrong, jnp.where(table[a * group:(a + 1) * group] == expected, 0.0, 1.0)
         )
-    flag_ref[0, 0] = jnp.max(wrong)
+    flag_ref[...] = jnp.broadcast_to(
+        jnp.max(jnp.max(wrong, axis=0, keepdims=True), axis=1, keepdims=True), flag_ref.shape
+    )
+    verdict = pltpu.make_async_copy(flag_ref, flag_hbm, fetch_sems.at[len(fetches)])
+    verdict.start()
     pd_ref[:group, :] = base
     places = jnp.where(
         low_half, pd_ref[pl.ds(0, wraps, stride=2), :], pd_ref[pl.ds(1, wraps, stride=2), :]
@@ -582,7 +586,9 @@
         store_pair(ends_ref, group, w, found[0], found[slabs])
 
     def gather_inner():
-        gather(2 * block, tuple(range(1, slabs)), inner_found, 1)
+        @pl.when(me >= 0)
+        def split():
+            gather(2 * block, tuple(range(1, slabs)), inner_found, 1)
 
     def gather_outer():
         gather(0, (0, slabs), outer_found, 1)
@@ -802,6 +808,7 @@
     put_psi(slabs, ghost_ref, 0)
     gather_outer()
     copies = send_atoms(0, partial_outer(accs))
+    verdict.wait()
     potf_ref[slabs * rows128:slabs * rows128 + potg_ref.shape[0], :] = (
         potg_ref[...].astype(F32) - CENTER
     )
@@ -856,8 +863,9 @@
 
     def last_done(a, layer, out):
         last_layer(layer, lambda t: out[t])
-        if layer >= half:
-            swap(a, jnp.where(band == 0, a + half, a) if a else half).start()
+        if layer >= half and a in (half // 2, half - 1):
+            for n in range(0 if a == half // 2 else half // 2 + 1, a + 1):
+                swap(n, jnp.where(band == 0, n + half, n) if n else half).start()
 
     scatter_rest(terms, last_done)
 
@@ -1028,6 +1036,17 @@
     return (filtered, correlation)
 
 
+def hand_over(filtered_ref, correlation_ref, out_ref, corr_ref, sems):
+    copies = [
+        pltpu.make_async_copy(filtered_ref, out_ref, sems.at[0]),
+        pltpu.make_async_copy(correlation_ref, corr_ref, sems.at[1]),
+    ]
+    for copy in copies:
+        copy.start()
+    for copy in copies:
+        copy.wait()
+
+
 def bricks(states, node_count, width, cells, bands):
     edge = round(width ** (1.0 / 3.0))
     return (
@@ -1074,7 +1093,6 @@
     ghost_rows = (FACEP // 128 + 15) // 16 * 16
     size = bands * states
     vmem = pl.BlockSpec(memory_space=pltpu.VMEM)
-    smem = pl.BlockSpec(memory_space=pltpu.SMEM)
     anywhere = pl.BlockSpec(memory_space=pl.ANY)
     face = (states, FACEP)
     duo = (nproj * states, 2 * atoms)
@@ -1083,11 +1101,12 @@
         out_shape=(
             jax.ShapeDtypeStruct((states, node_count), BF16),
             jax.ShapeDtypeStruct((size, size), F32),
-            jax.ShapeDtypeStruct((1, 1), F32),
+            jax.ShapeDtypeStruct((1, 128), F32),
         ),
         in_specs=[anywhere] * 9,
-        out_specs=(vmem, vmem, smem),
+        out_specs=(vmem, vmem, anywhere),
         scratch_shapes=[
+            pltpu.VMEM((1, 128), F32),
             pltpu.VMEM(psi.shape, BF16),
             pltpu.VMEM(cell_nodes.shape, jnp.int32),
             pltpu.VMEM(cell_matrix.shape, BF16),
@@ -1129,7 +1148,7 @@
             pltpu.VMEM(face, F32),
             pltpu.VMEM(face, F32),
             pltpu.VMEM(((width + 4 * wraps) * nproj, entries), F32),
-            pltpu.SemaphoreType.DMA((9,)),
+            pltpu.SemaphoreType.DMA((10,)),
             pltpu.SemaphoreType.DMA((2, 26)),
         ],
         compiler_params=pltpu.CompilerParams(collective_id=0, has_side_effects=True),
@@ -1140,11 +1159,19 @@
         entry_atom.reshape(1, entries),
         coupling.transpose(1, 2, 0).reshape(nproj * nproj, atoms),
     )
-    return lax.cond(
+    results = lax.cond(
         wrong[0, 0] > 0.0,
         lambda: general(*operands),
         lambda: (filtered, correlation),
     )
+    return pl.pallas_call(
+        hand_over,
+        out_shape=tuple(jax.ShapeDtypeStruct(one.shape, one.dtype) for one in results),
+        in_specs=[anywhere] * 2,
+        out_specs=(anywhere,) * 2,
+        scratch_shapes=[pltpu.SemaphoreType.DMA((2,))],
+        name="hand_over",
+    )(*results)
 
 
 def solution(mesh):

time: 42.5 us -> 42.1 us (level)
  local copies, waits for them, and re-layouts: 1.35 us -> 0.04 us
  Pallas kernels: 39.4 us -> 40.2 us
    unnamed x20 -> x18, local copies, waits for them, and re-layouts: 1.35 us -> 0.04 us
    pallas_call x0 -> x1, Pallas kernels: none -> 0.73 us  [local(): pl.pallas_call(hand_over, out_shape=tuple((jax.ShapeDtypeStruct(one.shape...]
where the time goes in v5:
time: 42.1 us; the launch traced here: 41.9 us
  Pallas kernels  40.2 us (95%)
  between operations  1.51 us (4%)
    pallas_call x1, Pallas kernels, local(): pl.pallas_call(fused_kernel, out_shape=(jax.ShapeDtypeStruct((states, nod...  39.5 us

profile of v5, /device:TPU:0, one launch (start us, length us, event | category | flops | bytes accessed | tf_op | source)
XLA Modules:
  0.0 41.9 jit_solution(14844421174609337473)
XLA Ops:
  0.6 0.0 copy-start.6
  0.6 0.0 copy-start.8
  0.7 0.0 copy-start.7
  0.7 0.0 copy-start
  0.7 0.0 copy-start.5
  0.7 0.0 copy-start.3
  0.7 0.0 copy-start.9
  0.7 0.0 copy-start.4
  0.7 0.0 copy-start.2
  0.7 39.5 %fused_steps.1 = (bf16[8,17920]{1,0:T(8,128)(2,1)S(1)}, f32[16,16]{1,0:T(8,128)S(1)}, f32[1,128]{1,0:T(1,128)}) custom-call(bf16[8,17920]{1,0:T(8,128)(2,1)} %psi_hbm.1, s32[216,128]{1,0:T(8,128)} %cn_hbm.1, f32[1,128]{1,0:T(1,128)} %bitcast.30, bf16[216,216]{1,0:T(8,128)(2,1)} %kmat_hbm.1, bf16[140,128]{1,0:T(8,128)(2,1)} %bitcast.17, ...), custom_call_target="tpu_custom_call" | custom-call | tf_op jit(solution)/shard_map/fused_steps/pallas_call | solution.py:1099
  40.8 0.0 copy-done.6
  40.8 0.0 copy-done.8
  40.8 0.0 copy-done.7
  40.8 0.0 copy-done
  40.8 0.0 copy-done.5
  40.8 0.0 copy-done.3
  40.8 0.0 copy-done.9
  40.8 0.0 copy-done.4
  40.8 0.0 copy-done.2
  40.8 0.2 conditional.1
  41.0 0.7 %hand_over.1 = (bf16[8,17920]{1,0:T(8,128)(2,1)}, f32[16,16]{1,0:T(8,128)}) custom-call(bf16[8,17920]{1,0:T(8,128)(2,1)S(1)} %get-tuple-element.48.filtered_ref, f32[16,16]{1,0:T(8,128)S(1)} %get-tuple-element.49.correlation_ref), custom_call_target="tpu_custom_call" | custom-call | tf_op jit(solution)/shard_map/hand_over/pallas_call | solution.py:1167
Async XLA Ops:
  0.6 40.1 %copy-start.6 = (f32[64,8,8]{0,2,1:T(8,128)S(1)}, f32[64,8,8]{0,2,1:T(8,128)}, u32[]{:S(2)}) copy-start(f32[64,8,8]{0,2,1:T(8,128)} %param.19) | copy-start | bytes 49156
  0.6 40.1 %copy-start.8 = (s32[128]{0:T(128)S(1)}, s32[128]{0:T(128)}, u32[]{:S(2)}) copy-start(s32[128]{0:T(128)} %param.18) | copy-start | bytes 1540
  0.7 40.1 %copy-start.7 = (s32[128]{0:T(128)S(1)}, s32[128]{0:T(128)}, u32[]{:S(2)}) copy-start(s32[128]{0:T(128)} %param.17) | copy-start | bytes 1540
  0.7 40.1 %copy-start = (bf16[216,8,128]{2,1,0:T(8,128)(2,1)S(1)}, bf16[216,8,128]{2,1,0:T(8,128)(2,1)}, u32[]{:S(2)}) copy-start(bf16[216,8,128]{2,1,0:T(8,128)(2,1)} %proj_hbm.1) | copy-start | bytes 1327108
  0.7 40.1 %copy-start.5 = (bf16[17920]{0:T(1024)(128)(2,1)S(1)}, bf16[17920]{0:T(1024)(128)(2,1)}, u32[]{:S(2)}) copy-start(bf16[17920]{0:T(1024)(128)(2,1)} %param.15) | copy-start | bytes 107524
  0.7 40.1 %copy-start.3 = (bf16[216,216]{1,0:T(8,128)(2,1)S(1)}, bf16[216,216]{1,0:T(8,128)(2,1)}, u32[]{:S(2)}) copy-start(bf16[216,216]{1,0:T(8,128)(2,1)} %kmat_hbm.1) | copy-start | bytes 279940
  0.7 40.1 %copy-start.9 = (f32[128]{0:T(128)S(1)}, f32[128]{0:T(128)}, u32[]{:S(2)}) copy-start(f32[128]{0:T(128)} %param.13) | copy-start | bytes 1540
  0.7 40.1 %copy-start.4 = (s32[216,128]{1,0:T(8,128)S(1)}, s32[216,128]{1,0:T(8,128)}, u32[]{:S(2)}) copy-start(s32[216,128]{1,0:T(8,128)} %cn_hbm.1) | copy-start | bytes 331780
  0.7 40.1 %copy-start.2 = (bf16[8,17920]{1,0:T(8,128)(2,1)S(1)}, bf16[8,17920]{1,0:T(8,128)(2,1)}, u32[]{:S(2)}) copy-start(bf16[8,17920]{1,0:T(8,128)(2,1)} %psi_hbm.1) | copy-start | bytes 860164

commit v6 on v5

--- a/solution.py
+++ b/solution.py
@@ -407,11 +407,26 @@
     ahead_mate = {"mesh": ring_peer(1), "band": lax.rem(band + 1, bands)}
     barrier = pltpu.get_barrier_semaphore()
 
-    def greet_body(steps, carry):
-        pl.semaphore_signal(barrier, inc=1, device_id=peer(steps), device_id_type=MESH_ID)
-        return carry
-
-    lax.fori_loop(0, devices * bands - 1, greet_body, 0)
+    behind_mate = {"mesh": ring_peer(-1), "band": lax.rem(band + 1, bands)}
+    if devices > 16:
+        guests = devices * bands - 1
+
+        def greet_body(n, carry):
+            pl.semaphore_signal(barrier, inc=1, device_id=peer(n), device_id_type=MESH_ID)
+            return carry
+
+        lax.fori_loop(0, guests, greet_body, 0)
+    else:
+        near = (ahead, behind, ahead2, behind2, ahead_mate, behind_mate, partner)
+        guests = len(near)
+        for one in near:
+            pl.semaphore_signal(barrier, inc=1, device_id=one, device_id_type=MESH_ID)
+    part = face // 2
+    own_part, mate_part = band * part, (bands - 1 - band) * part
+
+    def span(at, size):
+        return pl.ds(pl.multiple_of(at, 128), size)
+
     for fetch in fetches[:4]:
         fetch.wait()
     down = lax.broadcasted_iota(jnp.int32, (cells, cells), 0)
@@ -475,13 +490,13 @@
                 jnp.where(hi == t, 1.0, 0.0).astype(BF16)
             )
     coups_ref[1] = jnp.concatenate([coup_ref[...]] * 2, axis=1)
-    pl.semaphore_wait(barrier, devices * bands - 1)
+    pl.semaphore_wait(barrier, guests)
     gaps = [
         send(psi_hbm.at[:, :face], ghost_ref, sems, 0, behind),
         send(pot_hbm.at[:potg_ref.shape[0], :], potg_ref, sems, 1, behind),
         send(coups_ref.at[1], coups_ref.at[0], sems, 2, ahead),
         send(coups_ref.at[1], coups_ref.at[2], sems, 3, behind),
-        send(psi_hbm.at[:, :face], mate_ref, sems, 18, partner),
+        send(psi_hbm.at[:, span(mate_part, part)], mate_ref, sems, 18, partner),
     ]
 
     rows128 = face // 128
@@ -837,7 +852,7 @@
     )
     gather_outer()
     copies = send_atoms(1, partial_outer(accs))
-    mated = [send(first_ref.at[:, :face], mated_ref, sems, 20, partner)]
+    mated = [send(first_ref.at[:, span(mate_part, part)], mated_ref, sems, 20, partner)]
     cell_terms()
     for copy in copies:
         copy.wait()
@@ -845,18 +860,19 @@
     scatter_outer(1, terms)
     tails = [
         send(tail_ref.at[1], low_ref.at[1], sems, 14, ahead),
-        send(tail_ref.at[1], matel_ref, sems, 16, ahead_mate),
-        send(head_ref.at[1], mateh_ref, sems, 19, partner),
+        send(tail_ref.at[1, :, span(mate_part, part)], matel_ref, sems, 16, ahead_mate),
+        send(head_ref.at[1, :, span(mate_part, part)], mateh_ref, sems, 19, partner),
     ]
     half = edge - 1
 
-    def span(at, size):
-        return pl.ds(pl.multiple_of(at, 128), size)
-
-    def swap(n, layer):
+    def swap(n):
+        if n == 0:
+            at, size = half * face + mate_part, part
+        else:
+            at, size = jnp.where(band == 0, n + half, n) * face, face
         return pltpu.make_async_remote_copy(
-            src_ref=out_ref.at[:, span(layer * face, face)],
-            dst_ref=other_ref.at[:, span(n * face, face)],
+            src_ref=out_ref.at[:, span(at, size)],
+            dst_ref=other_ref.at[:, span(n * face, size)],
             send_sem=sems.at[0, 21 + n], recv_sem=sems.at[1, 21 + n],
             device_id=partner, device_id_type=MESH_ID,
         )
@@ -865,7 +881,7 @@
         last_layer(layer, lambda t: out[t])
         if layer >= half and a in (half // 2, half - 1):
             for n in range(0 if a == half // 2 else half // 2 + 1, a + 1):
-                swap(n, jnp.where(band == 0, n + half, n) if n else half).start()
+                swap(n).start()
 
     scatter_rest(terms, last_done)
 
@@ -875,10 +891,12 @@
         ).astype(BF16)
         return lax.dot_general(both, both, back, preferred_element_type=F32)
 
-    swap(0, half).wait()
-    total = jnp.zeros((bands * states, bands * states), F32)
+    swap(0).wait()
+    total = gram(
+        out_ref[:, span(half * face + own_part, part)].astype(F32), other_ref[:, :part].astype(F32)
+    )
     for n in range(1, half):
-        swap(n, half).wait()
+        swap(n).wait()
         total = total + gram(
             out_ref[:, span(jnp.where(band == 0, n, n + half) * face, face)].astype(F32),
             other_ref[:, n * face:(n + 1) * face].astype(F32),
@@ -887,15 +905,13 @@
         copy.wait()
     last_layer(0, edge_sum(head_ref.at[1], low_ref.at[1]))
     blocks = []
-    summed = edge_sum(mateh_ref, matel_ref)
-    for t in range(tiles):
-        at = slice(t * WIDE, (t + 1) * WIDE)
-        value = scaled(0, t, summed(t), mated_ref[:, at])
-        value = (2.0 * value - mate_ref[:, at].astype(F32)).astype(BF16).astype(F32)
-        blocks.append(jnp.where(band == 0, value, other_ref[:, at].astype(F32)))
+    for t in range(part // 128):
+        at = slice(t * 128, (t + 1) * 128)
+        pot = potf_ref[pl.ds(band * (part // 128) + t, 1), :]
+        value = (mateh_ref[:, at] + matel_ref[:, at] + pot * mated_ref[:, at]) * (1.0 / HALFWIDTH)
+        blocks.append((2.0 * value - mate_ref[:, at].astype(F32)).astype(BF16).astype(F32))
     total = total + gram(
-        out_ref[:, span(jnp.where(band == 0, 0, half) * face, face)].astype(F32),
-        jnp.concatenate(blocks, axis=1),
+        out_ref[:, span(own_part, part)].astype(F32), jnp.concatenate(blocks, axis=1)
     )
     size = bands * states
     lump = size * size // 128
@@ -1055,6 +1071,7 @@
         and edge % 2 == 0
         and cells == 128
         and FACEP % WIDE == 0
+        and FACEP % 256 == 0
         and states == 8
         and bands == 2
         and edge * edge % 6 == 0
@@ -1143,10 +1160,10 @@
             pltpu.VMEM((devices * bands, size * size // 128, 128), F32),
             pltpu.VMEM((per, wraps * cells), BF16),
             pltpu.VMEM((2, nproj * nproj, 2 * atoms), F32),
-            pltpu.VMEM(face, BF16),
-            pltpu.VMEM(face, F32),
-            pltpu.VMEM(face, F32),
-            pltpu.VMEM(face, F32),
+            pltpu.VMEM((states, FACEP // 2), BF16),
+            pltpu.VMEM((states, FACEP // 2), F32),
+            pltpu.VMEM((states, FACEP // 2), F32),
+            pltpu.VMEM((states, FACEP // 2), F32),
             pltpu.VMEM(((width + 4 * wraps) * nproj, entries), F32),
             pltpu.SemaphoreType.DMA((10,)),
             pltpu.SemaphoreType.DMA((2, 26)),

time: 42.1 us -> 40.8 us (0.969)
  Pallas kernels: 40.2 us -> 38.9 us
    pallas_call x1, Pallas kernels: 39.5 us -> 38.1 us  [local(): pl.pallas_call(fused_kernel, out_shape=(jax.ShapeDtypeStruct((states, nod...]
where the time goes in v6:
time: 40.8 us; the launch traced here: 40.6 us
  Pallas kernels  38.9 us (95%)
  between operations  1.51 us (4%)
    pallas_call x1, Pallas kernels, local(): pl.pallas_call(fused_kernel, out_shape=(jax.ShapeDtypeStruct((states, nod...  38.1 us

profile of v6, /device:TPU:0, one launch (start us, length us, event | category | flops | bytes accessed | tf_op | source)
XLA Modules:
  0.0 40.6 jit_solution(7225672907809821139)
XLA Ops:
  0.6 0.0 copy-start.6
  0.6 0.0 copy-start.8
  0.7 0.0 copy-start.7
  0.7 0.0 copy-start
  0.7 0.0 copy-start.5
  0.7 0.0 copy-start.3
  0.7 0.0 copy-start.9
  0.7 0.0 copy-start.4
  0.7 0.0 copy-start.2
  0.7 38.1 %fused_steps.1 = (bf16[8,17920]{1,0:T(8,128)(2,1)S(1)}, f32[16,16]{1,0:T(8,128)S(1)}, f32[1,128]{1,0:T(1,128)}) custom-call(bf16[8,17920]{1,0:T(8,128)(2,1)} %psi_hbm.1, s32[216,128]{1,0:T(8,128)} %cn_hbm.1, f32[1,128]{1,0:T(1,128)} %bitcast.30, bf16[216,216]{1,0:T(8,128)(2,1)} %kmat_hbm.1, bf16[140,128]{1,0:T(8,128)(2,1)} %bitcast.17, ...), custom_call_target="tpu_custom_call" | custom-call | tf_op jit(solution)/shard_map/fused_steps/pallas_call | solution.py:1116
  39.4 0.0 copy-done.6
  39.4 0.0 copy-done.8
  39.4 0.0 copy-done.7
  39.5 0.0 copy-done
  39.5 0.0 copy-done.5
  39.5 0.0 copy-done.3
  39.5 0.0 copy-done.9
  39.5 0.0 copy-done.4
  39.5 0.0 copy-done.2
  39.5 0.2 conditional.1
  39.7 0.7 %hand_over.1 = (bf16[8,17920]{1,0:T(8,128)(2,1)}, f32[16,16]{1,0:T(8,128)}) custom-call(bf16[8,17920]{1,0:T(8,128)(2,1)S(1)} %get-tuple-element.48.filtered_ref, f32[16,16]{1,0:T(8,128)S(1)} %get-tuple-element.49.correlation_ref), custom_call_target="tpu_custom_call" | custom-call | tf_op jit(solution)/shard_map/hand_over/pallas_call | solution.py:1184
Async XLA Ops:
  0.6 38.8 %copy-start.6 = (f32[64,8,8]{0,2,1:T(8,128)S(1)}, f32[64,8,8]{0,2,1:T(8,128)}, u32[]{:S(2)}) copy-start(f32[64,8,8]{0,2,1:T(8,128)} %param.19) | copy-start | bytes 49156
  0.6 38.8 %copy-start.8 = (s32[128]{0:T(128)S(1)}, s32[128]{0:T(128)}, u32[]{:S(2)}) copy-start(s32[128]{0:T(128)} %param.18) | copy-start | bytes 1540
  0.7 38.8 %copy-start.7 = (s32[128]{0:T(128)S(1)}, s32[128]{0:T(128)}, u32[]{:S(2)}) copy-start(s32[128]{0:T(128)} %param.17) | copy-start | bytes 1540
  0.7 38.8 %copy-start = (bf16[216,8,128]{2,1,0:T(8,128)(2,1)S(1)}, bf16[216,8,128]{2,1,0:T(8,128)(2,1)}, u32[]{:S(2)}) copy-start(bf16[216,8,128]{2,1,0:T(8,128)(2,1)} %proj_hbm.1) | copy-start | bytes 1327108
  0.7 38.8 %copy-start.5 = (bf16[17920]{0:T(1024)(128)(2,1)S(1)}, bf16[17920]{0:T(1024)(128)(2,1)}, u32[]{:S(2)}) copy-start(bf16[17920]{0:T(1024)(128)(2,1)} %param.15) | copy-start | bytes 107524
  0.7 38.8 %copy-start.3 = (bf16[216,216]{1,0:T(8,128)(2,1)S(1)}, bf16[216,216]{1,0:T(8,128)(2,1)}, u32[]{:S(2)}) copy-start(bf16[216,216]{1,0:T(8,128)(2,1)} %kmat_hbm.1) | copy-start | bytes 279940
  0.7 38.8 %copy-start.9 = (f32[128]{0:T(128)S(1)}, f32[128]{0:T(128)}, u32[]{:S(2)}) copy-start(f32[128]{0:T(128)} %param.13) | copy-start | bytes 1540
  0.7 38.8 %copy-start.4 = (s32[216,128]{1,0:T(8,128)S(1)}, s32[216,128]{1,0:T(8,128)}, u32[]{:S(2)}) copy-start(s32[216,128]{1,0:T(8,128)} %cn_hbm.1) | copy-start | bytes 331780
  0.7 38.8 %copy-start.2 = (bf16[8,17920]{1,0:T(8,128)(2,1)S(1)}, bf16[8,17920]{1,0:T(8,128)(2,1)}, u32[]{:S(2)}) copy-start(bf16[8,17920]{1,0:T(8,128)(2,1)} %psi_hbm.1) | copy-start | bytes 860164

commit v7 on v6

--- a/solution.py
+++ b/solution.py
@@ -744,15 +744,16 @@
         for w, (one, two) in enumerate(node_rows(width * nproj, before, terms)):
             fill(2 * per, w, one + two)
 
-    def fill_inner(a, terms):
+    def fill_inner(a, terms, one_at, two_at):
         found = node_rows(a * group * nproj, terms_at(a), terms)
         for w, (one, two) in enumerate(found):
-            fill((2 * a + 1) * per, w, one)
-            fill((2 * a + 2) * per, w, two)
+            fill(one_at * per, w, one)
+            fill(two_at * per, w, two)
 
     def scatter(into, number):
+        into = into if isinstance(into, int) else pl.multiple_of(into, per)
         out = jnp.dot(
-            masked_ref[into:into + number * per, :], oht_ref[...], preferred_element_type=F32
+            masked_ref[pl.ds(into, number * per), :], oht_ref[...], preferred_element_type=F32
         )
         return [
             [joined(out[n * per:(n + 1) * per], t) for t in range(tiles)] for n in range(number)
@@ -774,7 +775,7 @@
         fill_early(terms)
         for a in range(1, edge):
             if a < edge - 1:
-                fill_inner(a, terms)
+                fill_inner(a, terms, 2 * a + 1, 2 * a + 2)
             if a == 1:
                 (out,) = scatter(2 * per, 1)
                 finish(0, edge - 1, out)
@@ -877,13 +878,33 @@
             device_id=partner, device_id_type=MESH_ID,
         )
 
-    def last_done(a, layer, out):
-        last_layer(layer, lambda t: out[t])
-        if layer >= half and a in (half // 2, half - 1):
-            for n in range(0 if a == half // 2 else half // 2 + 1, a + 1):
-                swap(n).start()
-
-    scatter_rest(terms, last_done)
+    def sent(a):
+        return jnp.where(band == 0, a + half, a)
+
+    def kept(a):
+        return jnp.where(band == 0, a, a + half)
+
+    def finish(first, number, rows, layer_of):
+        found = scatter(rows * per, number)
+        for n in range(number):
+            last_layer(layer_of(first + n), lambda t: found[n][t])
+
+    upper, lower = edge + 1, 3
+    sent_rows = jnp.where(band == 0, upper, lower)
+    kept_rows = jnp.where(band == 0, lower, upper)
+    early_half = (half - 1) // 2
+    fill_early(terms)
+    for a in range(1, half):
+        fill_inner(a, terms, lower + a - 1, upper + a - 1)
+        if a == early_half:
+            finish(0, 1, 2, lambda a: half)
+            finish(1, early_half, sent_rows, sent)
+    for n in range(early_half + 1):
+        swap(n).start()
+    finish(early_half + 1, half - 1 - early_half, sent_rows + early_half, sent)
+    for n in range(early_half + 1, half):
+        swap(n).start()
+    finish(1, half - 1, kept_rows, kept)
 
     def gram(own, other):
         both = jnp.concatenate(

time: 40.8 us -> 40.7 us (level)
  no operation moved by 1% of the time
where the time goes in v7:
time: 40.7 us; the launch traced here: 40.6 us
  Pallas kernels  38.8 us (95%)
  between operations  1.51 us (4%)
    pallas_call x1, Pallas kernels, local(): pl.pallas_call(fused_kernel, out_shape=(jax.ShapeDtypeStruct((states, nod...  38.1 us

profile of v7, /device:TPU:0, one launch (start us, length us, event | category | flops | bytes accessed | tf_op | source)
XLA Modules:
  0.0 40.6 jit_solution(6113344946176281472)
XLA Ops:
  0.6 0.0 copy-start.6
  0.6 0.0 copy-start.8
  0.7 0.0 copy-start.7
  0.7 0.0 copy-start
  0.7 0.0 copy-start.5
  0.7 0.0 copy-start.3
  0.7 0.0 copy-start.9
  0.7 0.0 copy-start.4
  0.7 0.0 copy-start.2
  0.7 38.1 %fused_steps.1 = (bf16[8,17920]{1,0:T(8,128)(2,1)S(1)}, f32[16,16]{1,0:T(8,128)S(1)}, f32[1,128]{1,0:T(1,128)}) custom-call(bf16[8,17920]{1,0:T(8,128)(2,1)} %psi_hbm.1, s32[216,128]{1,0:T(8,128)} %cn_hbm.1, f32[1,128]{1,0:T(1,128)} %bitcast.30, bf16[216,216]{1,0:T(8,128)(2,1)} %kmat_hbm.1, bf16[140,128]{1,0:T(8,128)(2,1)} %bitcast.17, ...), custom_call_target="tpu_custom_call" | custom-call | tf_op jit(solution)/shard_map/fused_steps/pallas_call | solution.py:1137
  39.4 0.0 copy-done.6
  39.4 0.0 copy-done.8
  39.4 0.0 copy-done.7
  39.4 0.0 copy-done
  39.4 0.0 copy-done.5
  39.4 0.0 copy-done.3
  39.4 0.0 copy-done.9
  39.4 0.0 copy-done.4
  39.5 0.0 copy-done.2
  39.5 0.2 conditional.1
  39.7 0.7 %hand_over.1 = (bf16[8,17920]{1,0:T(8,128)(2,1)}, f32[16,16]{1,0:T(8,128)}) custom-call(bf16[8,17920]{1,0:T(8,128)(2,1)S(1)} %get-tuple-element.48.filtered_ref, f32[16,16]{1,0:T(8,128)S(1)} %get-tuple-element.49.correlation_ref), custom_call_target="tpu_custom_call" | custom-call | tf_op jit(solution)/shard_map/hand_over/pallas_call | solution.py:1205
Async XLA Ops:
  0.6 38.7 %copy-start.6 = (f32[64,8,8]{0,2,1:T(8,128)S(1)}, f32[64,8,8]{0,2,1:T(8,128)}, u32[]{:S(2)}) copy-start(f32[64,8,8]{0,2,1:T(8,128)} %param.19) | copy-start | bytes 49156
  0.6 38.7 %copy-start.8 = (s32[128]{0:T(128)S(1)}, s32[128]{0:T(128)}, u32[]{:S(2)}) copy-start(s32[128]{0:T(128)} %param.18) | copy-start | bytes 1540
  0.7 38.7 %copy-start.7 = (s32[128]{0:T(128)S(1)}, s32[128]{0:T(128)}, u32[]{:S(2)}) copy-start(s32[128]{0:T(128)} %param.17) | copy-start | bytes 1540
  0.7 38.7 %copy-start = (bf16[216,8,128]{2,1,0:T(8,128)(2,1)S(1)}, bf16[216,8,128]{2,1,0:T(8,128)(2,1)}, u32[]{:S(2)}) copy-start(bf16[216,8,128]{2,1,0:T(8,128)(2,1)} %proj_hbm.1) | copy-start | bytes 1327108
  0.7 38.7 %copy-start.5 = (bf16[17920]{0:T(1024)(128)(2,1)S(1)}, bf16[17920]{0:T(1024)(128)(2,1)}, u32[]{:S(2)}) copy-start(bf16[17920]{0:T(1024)(128)(2,1)} %param.15) | copy-start | bytes 107524
  0.7 38.7 %copy-start.3 = (bf16[216,216]{1,0:T(8,128)(2,1)S(1)}, bf16[216,216]{1,0:T(8,128)(2,1)}, u32[]{:S(2)}) copy-start(bf16[216,216]{1,0:T(8,128)(2,1)} %kmat_hbm.1) | copy-start | bytes 279940
  0.7 38.7 %copy-start.9 = (f32[128]{0:T(128)S(1)}, f32[128]{0:T(128)}, u32[]{:S(2)}) copy-start(f32[128]{0:T(128)} %param.13) | copy-start | bytes 1540
  0.7 38.7 %copy-start.4 = (s32[216,128]{1,0:T(8,128)S(1)}, s32[216,128]{1,0:T(8,128)}, u32[]{:S(2)}) copy-start(s32[216,128]{1,0:T(8,128)} %cn_hbm.1) | copy-start | bytes 331780
  0.7 38.7 %copy-start.2 = (bf16[8,17920]{1,0:T(8,128)(2,1)S(1)}, bf16[8,17920]{1,0:T(8,128)(2,1)}, u32[]{:S(2)}) copy-start(bf16[8,17920]{1,0:T(8,128)(2,1)} %psi_hbm.1) | copy-start | bytes 860164
